TPU v7x, 512 devices: a whole 4x4x16 slice. The times are simulated.
512 devices in a mesh: traj: 64 (over x, z_lo, core), lat: 8 (over z_hi, y).
Axes of the slice: x: 4, y: 4, z: 16 (z_hi: 2, z_lo: 8; z = z_hi * 8 + z_lo), core: 2. Of those that a mesh axis runs over, the one named last changes fastest.
Arguments:
- ensemble: float32 [64, 56, 192, 384], P('traj', None, 'lat'), may hold values from -4 to 4
- counts: int32 [64], P('traj'), may hold values from 0 to 4, as said below
- mixing: bfloat16 [56, 56], replicated, may hold values from -0.75 to 0.75
- weights: float32 [192], P('lat'), may hold values from 0.5 to 1.5
- legendre: bfloat16 [128, 192, 128], P('lat'), may hold values from -0.5 to 0.5
- to_modes: float32 [56, 56], replicated, may hold values from -0.75 to 0.75
- from_modes: float32 [56, 56], replicated, may hold values from -0.75 to 0.75
- mode_rates: float32 [56], replicated, may hold values from 0.1 to 10
Outputs:
- advanced: float32 [64, 56, 192, 384], P('traj', None, 'lat')
Inputs may be any that keep to these rules, and one draw needn't show every extreme that they name: The counts of all members sum to 64, and some member has exactly 4.
All inputs are finite; a program needn't handle non-finite values.
Results may differ from a plain program's by a relative error of at most 0.015.
Values may be sent and summed in bfloat16 or wider, within the bound.
No kernel may reach another device: no remote copies, remote signals or barrier semaphores. Data moves between devices by JAX's collectives and lax.ppermute only.
A program may use at most 64 MiB of HBM per device.

v0:
```python
import math

import jax
import jax.numpy as jnp
from jax import lax
from jax.sharding import PartitionSpec as P

time_step = 0.3
cubic_rate = 0.1


def clone_sources(counts):
    living = (counts > 0).astype(jnp.int32)
    surplus_end = jnp.cumsum(jnp.maximum(counts - 1, 0), dtype=jnp.int32)
    killed_rank = jnp.cumsum(1 - living, dtype=jnp.int32) - (1 - living)
    pulled = jnp.sum(
        (surplus_end[None, :] <= killed_rank[:, None]).astype(jnp.int32), axis=1, dtype=jnp.int32
    )
    members = jnp.arange(counts.shape[0], dtype=jnp.int32)
    return jnp.where(living > 0, members, pulled)


def fourier_tables(wavenumber, component, longitudes):
    positions = jnp.arange(longitudes, dtype=jnp.int32)
    product_index = positions[:, None] * wavenumber[None, :] % longitudes
    angles = 2.0 * math.pi / longitudes * product_index.astype(jnp.float32)
    signed = jnp.where(component[None, :] == 0, jnp.cos(angles), -jnp.sin(angles))
    factor = jnp.where(wavenumber == 0, 1.0, 2.0).astype(jnp.float32)
    return (signed.astype(jnp.bfloat16), (factor[None, :] * signed).T.astype(jnp.bfloat16))


def mode_divisor(mode_rates, degree_count):
    degrees = jnp.arange(degree_count, dtype=jnp.float32)
    degree_ratio = degrees * (degrees + 1.0) / (degree_count * (degree_count + 1.0))
    return 1.0 + mode_rates[:, None] * degree_ratio[None, :]


def grid_section(state_grid, mixing, lat_scale, forward):
    level_count, row_count, col_count = state_grid.shape
    rounded = state_grid.astype(jnp.bfloat16)
    mixing_term = jnp.dot(
        mixing,
        rounded.reshape(level_count, row_count * col_count),
        preferred_element_type=jnp.float32,
    ).reshape(level_count, row_count, col_count)
    tendency = state_grid + time_step * (
        mixing_term - cubic_rate * state_grid * state_grid * state_grid
    )
    grid_rounded = tendency.astype(jnp.bfloat16).reshape(level_count * row_count, col_count)
    fourier_sums = jnp.dot(grid_rounded, forward, preferred_element_type=jnp.float32)
    fourier_sums = fourier_sums.reshape(level_count, row_count, forward.shape[1])
    return (fourier_sums * lat_scale[None, :, None]).astype(jnp.bfloat16)


def implicit_solve(spectral, to_modes, from_modes, divisor):
    modal = (
        jnp.einsum("kl,pmln->pmkn", to_modes, spectral, precision=lax.Precision.HIGHEST)
        / divisor[None, None]
    )
    return jnp.einsum("lk,pmkn->pmln", from_modes, modal, precision=lax.Precision.HIGHEST).astype(
        jnp.bfloat16
    )


def local(ensemble, counts, mixing, weights, legendre, to_modes, from_modes, mode_rates):
    traj_count = lax.axis_size("traj")
    lat_count = lax.axis_size("lat")
    local_waves = legendre.shape[0]
    degree_count = legendre.shape[2]
    total_waves = local_waves * lat_count
    longitudes = ensemble.shape[3]
    columns = jnp.arange(2 * total_waves, dtype=jnp.int32)
    within = columns % (2 * local_waves)
    wavenumber = columns // (2 * local_waves) * local_waves + within % local_waves
    component = within // local_waves
    forward, backward = fourier_tables(wavenumber, component, longitudes)
    lat_scale = weights / longitudes
    divisor = mode_divisor(mode_rates, degree_count)
    sources = clone_sources(lax.all_gather(counts, "traj", axis=0, tiled=True))

    def to_spectral(received):
        split_parts = received.reshape(received.shape[0], received.shape[1], 2, local_waves)
        return jnp.einsum(
            "ljpm,mjn->pmln", split_parts, legendre, preferred_element_type=jnp.float32
        )

    def to_grid(received):
        flat_rows = received.reshape(received.shape[0] * received.shape[1], received.shape[2])
        result_grid = jnp.dot(flat_rows, backward, preferred_element_type=jnp.float32)
        return result_grid.reshape(received.shape[0], received.shape[1], longitudes)

    def to_implicit(coefficients):
        spectral = to_spectral(
            lax.all_to_all(coefficients, "lat", split_axis=2, concat_axis=1, tiled=True)
        )
        return implicit_solve(spectral, to_modes, from_modes, divisor)

    def to_band_grid(implicit):
        band_parts = jnp.einsum(
            "mjn,pmln->ljpm", legendre, implicit, preferred_element_type=jnp.float32
        )
        band_parts = band_parts.astype(jnp.bfloat16)
        band_parts = band_parts.reshape(band_parts.shape[0], band_parts.shape[1], 2 * local_waves)
        return to_grid(lax.all_to_all(band_parts, "lat", split_axis=1, concat_axis=2, tiled=True))

    state_grid = ensemble[0]
    own_implicit = to_implicit(grid_section(state_grid, mixing, lat_scale, forward))
    pieces = own_implicit.reshape(traj_count, own_implicit.size // traj_count)
    spread = lax.all_to_all(pieces, "traj", split_axis=0, concat_axis=0, tiled=True)
    chosen = jnp.take(spread, sources, axis=0)
    implicit = lax.all_to_all(chosen, "traj", split_axis=0, concat_axis=0, tiled=True).reshape(
        own_implicit.shape
    )
    state_grid = to_band_grid(implicit)
    state_grid = to_band_grid(to_implicit(grid_section(state_grid, mixing, lat_scale, forward)))
    return state_grid[None]


def solution(mesh):
    placed = (
        P("traj", None, "lat", None),
        P("traj"),
        P(),
        P("lat"),
        P("lat", None, None),
        P(),
        P(),
        P(),
    )
    return jax.shard_map(
        local, mesh=mesh, in_specs=placed, out_specs=P("traj", None, "lat", None), check_vma=False
    )
```

profile of v0, /device:TPU:34, one launch (start us, length us, event | category | flops | bytes accessed | tf_op | source)
XLA Modules:
  0.0 316.0 jit_solution(8870735721143674202)
XLA Ops:
  0.0 0.8 broadcast_multiply_fusion
  0.8 1.7 convert_element_type.74
  2.6 0.9 fusion.3
  3.5 2.1 fusion.12
  5.6 1.1 copy.132
  6.8 3.5 %reshape.265 = bf16[8,2,21504]{2,1,0:T(2,128)(2,1)} reshape(bf16[256,24,56]{2,1,0:T(8,128)(2,1)S(1)} %bitcast.126) | data formatting | bytes 1376256
  10.3 17.0 %all-to-all-start = ((bf16[8,2,21504]{2,1,0:T(2,128)(2,1)}), bf16[8,2,21504]{2,1,0:T(2,128)(2,1)S(1)}, u32[]{:S(2)}, u32[]{:S(2)}) async-start(bf16[8,2,21504]{2,1,0:T(2,128)(2,1)} %reshape.265), calls=%async_computation | async-start | bytes 1376256 | tf_op jit(solution)/shard_map/all_to_all | solution.py:94
  27.4 41.7 %all-to-all-done = bf16[8,2,21504]{2,1,0:T(2,128)(2,1)S(1)} async-done(((bf16[8,2,21504]{2,1,0:T(2,128)(2,1)}), bf16[8,2,21504]{2,1,0:T(2,128)(2,1)S(1)}, u32[]{:S(2)}, u32[]{:S(2)}) %all-to-all-start) | async-done | bytes 688160 | tf_op jit(solution)/shard_map/all_to_all | solution.py:94
  69.1 2.8 reshape.266
  72.2 0.9 fusion.14
  73.2 1.0 fusion.23
  74.2 1.0 fusion.24
  75.9 3.4 %reduce.3 = bf16[64,3584]{1,0:T(8,128)(2,1)S(1)} reduce(bf16[64,1,3584]{2,1,0:T(2,128)(2,1)S(1)} %all_to_all.72, bf16[]{:T(256)} %broadcast.309), dimensions={1}, to_apply=%all_to_all.72.reduce_sub_computation | reduce | bytes 917506 | tf_op jit(solution)/shard_map/all_to_all | solution.py:109
  79.4 0.9 reshape.267
  80.3 8.6 %all-to-all-start.1 = ((bf16[64,2,1792]{2,1,0:T(2,128)(2,1)}), bf16[64,2,1792]{2,1,0:T(2,128)(2,1)S(1)}, u32[]{:S(2)}, u32[]{:S(2)}) async-start(bf16[64,2,1792]{2,1,0:T(2,128)(2,1)} %reshape.267), calls=%async_computation.1 | async-start | bytes 917504 | tf_op jit(solution)/shard_map/all_to_all | solution.py:109
  89.5 1.3 dynamic-slice
  90.7 0.7 dynamic-update-slice
  91.4 28.6 %all-reduce = s32[64]{0:T(128)S(1)} all-reduce(s32[64]{0:T(128)S(1)} %dynamic-update-slice), channel_id=1, replica_groups=mesh['traj'=64,'lat'=8] {'traj'}, use_global_device_ids=true, to_apply=%add | all-reduce | flops 64 | bytes 512
  121.3 0.8 gather_fusion
  122.2 1.0 reduce.4
  123.3 37.0 %all_to_all.79 = bf16[64,2,1792]{2,1,0:T(2,128)(2,1)S(1)} all-to-all(bf16[64,2,1792]{2,1,0:T(2,128)(2,1)S(1)} %reshape.269), channel_id=1, replica_groups=mesh['traj'=64,'lat'=8] {'traj'}, dimensions={0} | all-to-all | bytes 917504 | tf_op jit(solution)/shard_map/all_to_all | solution.py:111
  160.7 2.7 reduce.2
  164.1 0.6 fusion.20
  165.0 2.1 copy.141
  167.1 3.5 %reshape.271 = bf16[8,2,21504]{2,1,0:T(2,128)(2,1)} reshape(bf16[192,32,56]{2,1,0:T(8,128)(2,1)S(1)} %bitcast.129) | data formatting | bytes 1376256
  170.7 3.9 %all-to-all-start.3 = ((bf16[8,2,21504]{2,1,0:T(2,128)(2,1)}), bf16[8,2,21504]{2,1,0:T(2,128)(2,1)S(1)}, u32[]{:S(2)}, u32[]{:S(2)}) async-start(bf16[8,2,21504]{2,1,0:T(2,128)(2,1)} %reshape.271), calls=%async_computation.3 | async-start | bytes 1376256 | tf_op jit(solution)/shard_map/all_to_all | solution.py:104
  174.6 41.6 %all-to-all-done.3 = bf16[8,2,21504]{2,1,0:T(2,128)(2,1)S(1)} async-done(((bf16[8,2,21504]{2,1,0:T(2,128)(2,1)}), bf16[8,2,21504]{2,1,0:T(2,128)(2,1)S(1)}, u32[]{:S(2)}, u32[]{:S(2)}) %all-to-all-start.3) | async-done | bytes 688160 | tf_op jit(solution)/shard_map/all_to_all | solution.py:104
  216.3 2.8 reshape.272
  219.1 1.6 copy.142
  220.7 1.8 copy.143
  222.5 2.2 fusion.92
  225.3 0.6 fusion.7
  226.0 2.1 fusion.13
  228.1 1.1 copy.150
  229.2 2.8 reshape.273
  232.1 30.2 %all_to_all.80 = bf16[8,2,21504]{2,1,0:T(2,128)(2,1)} all-to-all(bf16[8,2,21504]{2,1,0:T(2,128)(2,1)S(1)} %reshape.273), channel_id=1, replica_groups=mesh['traj'=64,'lat'=8] {'lat'}, dimensions={0} | all-to-all | bytes 1376256 | tf_op jit(solution)/shard_map/all_to_all | solution.py:94
  262.3 3.8 %reshape.274 = bf16[256,24,56]{2,1,0:T(8,128)(2,1)S(1)} reshape(bf16[8,2,21504]{2,1,0:T(2,128)(2,1)} %all_to_all.80) | data formatting | bytes 1376256
  266.4 0.9 fusion.17
  267.3 1.0 fusion.22
  268.3 1.0 fusion.25
  269.2 0.6 fusion.21
  270.2 2.1 copy.157
  272.3 2.8 reshape.275
  275.1 30.0 %all_to_all.81 = bf16[8,2,21504]{2,1,0:T(2,128)(2,1)} all-to-all(bf16[8,2,21504]{2,1,0:T(2,128)(2,1)S(1)} %reshape.275), channel_id=1, replica_groups=mesh['traj'=64,'lat'=8] {'lat'}, dimensions={0} | all-to-all | bytes 1376256 | tf_op jit(solution)/shard_map/all_to_all | solution.py:104
  305.1 3.8 %reshape.276 = bf16[192,32,56]{2,1,0:T(8,128)(2,1)S(1)} reshape(bf16[8,2,21504]{2,1,0:T(2,128)(2,1)} %all_to_all.81) | data formatting | bytes 1376256
  308.9 1.6 copy.158
  310.5 1.8 copy.159
  312.3 3.5 %convolution_bitcast_fusion = f32[1,56,24,384]{3,2,1,0:T(8,128)} fusion(bf16[56,24,256]{2,1,0:T(8,128)(2,1)S(1)} %copy.159, s32[256]{0:T(256)S(1)} %fusion.73, f32[256]{0:T(256)S(1)} %compare_select_fusion.1, pred[256]{0:T(512)(128)(4,1)S(1)} %fusion.75), kind=kOutput, calls=%fused_computation.11 | convolution fusion | flops 265519104 | bytes 2754816 | tf_op jit(solution)/shard_map/dot_general | solution.py:89
  (44 shorter events, 5.1 us)
Async XLA Ops:
  0.0 72.2 %copy-start = (bf16[16,192,128]{2,1,0:T(8,128)(2,1)S(1)}, bf16[16,192,128]{2,1,0:T(8,128)(2,1)}, u32[]{:S(2)}) copy-start(bf16[16,192,128]{2,1,0:T(8,128)(2,1)} %param.12) | copy-start | bytes 2359300
  0.0 2.6 copy-start.1
  0.0 2.6 copy-start.3
  6.7 20.6 %copy-start.4 = (f32[56]{0:T(128)S(1)}, f32[56]{0:T(128)}, u32[]{:S(2)}) copy-start(f32[56]{0:T(128)} %param.15) | copy-start | bytes 676
  10.3 58.8 %all-to-all-start = ((bf16[8,2,21504]{2,1,0:T(2,128)(2,1)}), bf16[8,2,21504]{2,1,0:T(2,128)(2,1)S(1)}, u32[]{:S(2)}, u32[]{:S(2)}) async-start(bf16[8,2,21504]{2,1,0:T(2,128)(2,1)} %reshape.265), calls=%async_computation | async-start | bytes 1376256 | tf_op jit(solution)/shard_map/all_to_all | solution.py:94
  72.2 1.0 copy-start.5
  73.2 1.0 copy-start.2
  80.3 40.6 %all-to-all-start.1 = ((bf16[64,2,1792]{2,1,0:T(2,128)(2,1)}), bf16[64,2,1792]{2,1,0:T(2,128)(2,1)S(1)}, u32[]{:S(2)}, u32[]{:S(2)}) async-start(bf16[64,2,1792]{2,1,0:T(2,128)(2,1)} %reshape.267), calls=%async_computation.1 | async-start | bytes 917504 | tf_op jit(solution)/shard_map/all_to_all | solution.py:109
  170.7 45.6 %all-to-all-start.3 = ((bf16[8,2,21504]{2,1,0:T(2,128)(2,1)}), bf16[8,2,21504]{2,1,0:T(2,128)(2,1)S(1)}, u32[]{:S(2)}, u32[]{:S(2)}) async-start(bf16[8,2,21504]{2,1,0:T(2,128)(2,1)} %reshape.271), calls=%async_computation.3 | async-start | bytes 1376256 | tf_op jit(solution)/shard_map/all_to_all | solution.py:104
where the time goes:
time: 321 us; the launch traced here: 316 us
  blocking collectives  126 us (39%)
  waiting for transfers between devices  83.3 us (26%)
  local copies, waits for them, and re-layouts  46.7 us (15%)
  starting transfers between devices  29.5 us (9%)
  matrix products  18.2 us (6%)
  other arithmetic  11.2 us (3%)
    all_to_all x1, waiting for transfers between devices, to_implicit(): lax.all_to_all(coefficients, 'lat', split_axis=2, concat_axis=1, tiled=True)  41.7 us
    all_to_all x1, waiting for transfers between devices, to_band_grid(): lax.all_to_all(band_parts, 'lat', split_axis=1, concat_axis=2, tiled=True)  41.6 us
    all_to_all x1, blocking collectives, local(): lax.all_to_all(chosen, 'traj', split_axis=0, concat_axis=0, tiled=True)  37 us
    all_to_all x1, blocking collectives, to_implicit(): lax.all_to_all(coefficients, 'lat', split_axis=2, concat_axis=1, tiled=True)  30.2 us
    all_to_all x1, blocking collectives, to_band_grid(): lax.all_to_all(band_parts, 'lat', split_axis=1, concat_axis=2, tiled=True)  30 us
    unnamed x29, local copies, waits for them, and re-layouts  29.7 us
    unnamed x1, blocking collectives  28.6 us
    all_to_all x1, starting transfers between devices, to_implicit(): lax.all_to_all(coefficients, 'lat', split_axis=2, concat_axis=1, tiled=True)  17 us
  transfers between devices with their start and end apart: 3, of which 2 were waited for; matrix products, arithmetic and copies ran while one was open for 1% of the time, Pallas kernels for 0%

commit v1 on v0

--- a/solution.py
+++ b/solution.py
@@ -3,21 +3,12 @@
 import jax
 import jax.numpy as jnp
 from jax import lax
+from jax.experimental import pallas as pl
+from jax.experimental.pallas import tpu as pltpu
 from jax.sharding import PartitionSpec as P
 
 time_step = 0.3
 cubic_rate = 0.1
-
-
-def clone_sources(counts):
-    living = (counts > 0).astype(jnp.int32)
-    surplus_end = jnp.cumsum(jnp.maximum(counts - 1, 0), dtype=jnp.int32)
-    killed_rank = jnp.cumsum(1 - living, dtype=jnp.int32) - (1 - living)
-    pulled = jnp.sum(
-        (surplus_end[None, :] <= killed_rank[:, None]).astype(jnp.int32), axis=1, dtype=jnp.int32
-    )
-    members = jnp.arange(counts.shape[0], dtype=jnp.int32)
-    return jnp.where(living > 0, members, pulled)
 
 
 def fourier_tables(wavenumber, component, longitudes):
@@ -35,7 +26,7 @@
     return 1.0 + mode_rates[:, None] * degree_ratio[None, :]
 
 
-def grid_section(state_grid, mixing, lat_scale, forward):
+def grid_tendency(state_grid, mixing):
     level_count, row_count, col_count = state_grid.shape
     rounded = state_grid.astype(jnp.bfloat16)
     mixing_term = jnp.dot(
@@ -46,10 +37,110 @@
     tendency = state_grid + time_step * (
         mixing_term - cubic_rate * state_grid * state_grid * state_grid
     )
-    grid_rounded = tendency.astype(jnp.bfloat16).reshape(level_count * row_count, col_count)
+    return tendency.astype(jnp.bfloat16)
+
+
+def mix_levels(matrix, grid):
+    level_count, row_count, col_count = grid.shape
+    flat = grid.reshape(level_count, row_count * col_count)
+    mixed = jnp.dot(matrix.astype(jnp.bfloat16), flat, preferred_element_type=jnp.float32)
+    return mixed.reshape(grid.shape)
+
+
+def grid_section(state_grid, mixing, lat_scale, forward):
+    level_count, row_count, col_count = state_grid.shape
+    grid_rounded = grid_tendency(state_grid, mixing).reshape(level_count * row_count, col_count)
     fourier_sums = jnp.dot(grid_rounded, forward, preferred_element_type=jnp.float32)
     fourier_sums = fourier_sums.reshape(level_count, row_count, forward.shape[1])
     return (fourier_sums * lat_scale[None, :, None]).astype(jnp.bfloat16)
+
+
+def contract(left, right, left_dim, right_dim):
+    return lax.dot_general(
+        left, right, (((left_dim,), (right_dim,)), ((), ())), preferred_element_type=jnp.float32
+    )
+
+
+def block_mask(rows, cols, test):
+    row = lax.broadcasted_iota(jnp.int32, (rows, cols), 0)
+    col = lax.broadcasted_iota(jnp.int32, (rows, cols), 1)
+    return test(row, col)
+
+
+def spread_kernel(count_ref, table_ref, grid_ref, scale_ref, out_ref):
+    wave_count, quarters, pair_rows, lanes = out_ref.shape
+    used = grid_ref.shape[0] // quarters
+    table = table_ref[...]
+    lane = lax.broadcasted_iota(jnp.int32, (wave_count * pair_rows, lanes), 1)
+    for quarter in range(quarters):
+        block = grid_ref[quarter * used : (quarter + 1) * used, :]
+        block = jnp.concatenate(
+            [block, jnp.zeros((lanes - used, block.shape[1]), block.dtype)], axis=0
+        )
+        sums = contract(table, block, 1, 1) * scale_ref[...]
+        sums = jnp.where(lane < used, sums, count_ref[0])
+        out_ref[:, quarter] = sums.astype(jnp.bfloat16).reshape(wave_count, pair_rows, lanes)
+
+
+def selection(count_row, size):
+    surplus = jnp.maximum(count_row - 1.0, 0.0).astype(jnp.bfloat16)
+    dead = jnp.where(count_row == 0.0, 1.0, 0.0).astype(jnp.bfloat16)
+    dead_all = jnp.broadcast_to(dead[0:1], (size, size))
+    surplus_all = jnp.broadcast_to(surplus[0:1], (size, size))
+
+    def ones_where(test):
+        return jnp.where(block_mask(size, size, test), 1.0, 0.0).astype(jnp.bfloat16)
+
+    upto = ones_where(lambda r, c: (r // 2 <= c // 2) & (r % 2 == 0))
+    before = ones_where(lambda r, c: (c // 2 < r // 2) & (c % 2 == 0))
+    same = ones_where(lambda r, c: r == c)
+    surplus_end = contract(surplus_all, upto, 1, 0)
+    killed_rank = contract(before, dead_all, 1, 1)
+    killed = contract(same, dead_all, 1, 1)
+    even = block_mask(size, size, lambda r, c: c % 2 == 0)
+    pulled = jnp.sum(
+        jnp.where(even & (surplus_end <= killed_rank), 1.0, 0.0), axis=1, keepdims=True
+    )
+    member = lax.broadcasted_iota(jnp.int32, (size, size), 0) // 2
+    source = jnp.where(killed > 0.5, jnp.broadcast_to(pulled, (size, size)), member.astype(jnp.float32))
+    picked = lax.broadcasted_iota(jnp.int32, (size, size), 1) // 2
+    parity = block_mask(size, size, lambda r, c: r % 2 == c % 2)
+    return jnp.where(parity & (picked.astype(jnp.float32) == source), 1.0, 0.0).astype(jnp.bfloat16)
+
+
+def wave_kernel(parts_ref, table_ref, turned_ref, inverse_ref, out_ref, wave_ref, band_ref):
+    lat_count, size, lanes = parts_ref.shape
+    modes, lat_rows, _ = wave_ref.shape
+    rows = lat_rows // lat_count
+    used = modes * rows
+    unit = jnp.where(block_mask(used + 8, lanes, lambda r, c: r == c), 1.0, 0.0).astype(jnp.bfloat16)
+    pick = None
+    for lat in range(lat_count):
+        turned = contract(unit, parts_ref[lat], 1, 1)
+        if lat == 0:
+            pick = selection(turned[used : used + 8], size)
+        for mode in range(modes):
+            wave_ref[mode, lat * rows : (lat + 1) * rows, :] = turned[mode * rows : (mode + 1) * rows]
+    table = table_ref[...]
+    turned_table = turned_ref[...]
+    for mode in range(modes):
+        spectral = contract(turned_table, wave_ref[mode].astype(jnp.bfloat16), 1, 0)
+        modal = (spectral * inverse_ref[:, mode : mode + 1]).astype(jnp.bfloat16)
+        band = contract(table, modal, 1, 0)
+        for lat in range(lat_count):
+            band_ref[lat, mode * rows : (mode + 1) * rows, :] = band[lat * rows : (lat + 1) * rows]
+    out_ref[...] = jnp.zeros(out_ref.shape, out_ref.dtype)
+    for lat in range(lat_count):
+        chosen = contract(pick, band_ref[lat].astype(jnp.bfloat16), 1, 1)
+        out_ref[lat, :, 0:used] = chosen.astype(jnp.bfloat16)
+
+
+def gather_kernel(parts_ref, table_ref, out_ref):
+    quarters = parts_ref.shape[0]
+    used = out_ref.shape[0] // quarters
+    for quarter in range(quarters):
+        sums = contract(parts_ref[quarter], table_ref[...], 0, 0)
+        out_ref[quarter * used : (quarter + 1) * used, :] = sums[:used].astype(jnp.bfloat16)
 
 
 def implicit_solve(spectral, to_modes, from_modes, divisor):
@@ -76,7 +167,8 @@
     forward, backward = fourier_tables(wavenumber, component, longitudes)
     lat_scale = weights / longitudes
     divisor = mode_divisor(mode_rates, degree_count)
-    sources = clone_sources(lax.all_gather(counts, "traj", axis=0, tiled=True))
+    vmem = pl.BlockSpec(memory_space=pltpu.VMEM)
+    smem = pl.BlockSpec(memory_space=pltpu.SMEM)
 
     def to_spectral(received):
         split_parts = received.reshape(received.shape[0], received.shape[1], 2, local_waves)
@@ -103,15 +195,70 @@
         band_parts = band_parts.reshape(band_parts.shape[0], band_parts.shape[1], 2 * local_waves)
         return to_grid(lax.all_to_all(band_parts, "lat", split_axis=1, concat_axis=2, tiled=True))
 
-    state_grid = ensemble[0]
-    own_implicit = to_implicit(grid_section(state_grid, mixing, lat_scale, forward))
-    pieces = own_implicit.reshape(traj_count, own_implicit.size // traj_count)
-    spread = lax.all_to_all(pieces, "traj", split_axis=0, concat_axis=0, tiled=True)
-    chosen = jnp.take(spread, sources, axis=0)
-    implicit = lax.all_to_all(chosen, "traj", split_axis=0, concat_axis=0, tiled=True).reshape(
-        own_implicit.shape
-    )
-    state_grid = to_band_grid(implicit)
+    level_count, row_count = ensemble.shape[1], ensemble.shape[2]
+    quarters = traj_count // local_waves
+    modes = level_count // quarters
+    used = modes * row_count
+    lanes = -(-(used + 1) // 128) * 128
+    pairs = jnp.arange(2 * total_waves, dtype=jnp.int32)
+    pair_wave = pairs // 2 % lat_count * local_waves + pairs // (2 * lat_count)
+    pair_forward, pair_backward = fourier_tables(pair_wave, pairs % 2, longitudes)
+    traj_index = lax.axis_index("traj")
+    own_table = lax.dynamic_index_in_dim(legendre, traj_index // quarters, 0, keepdims=False)
+    own_divisor = lax.dynamic_slice_in_dim(divisor, traj_index % quarters * modes, modes, 0)
+    own_inverse = (1.0 / own_divisor).T
+    lane_scale = jnp.pad(jnp.tile(lat_scale, modes), (0, lanes - used))[None, :]
+
+    grid_rounded = grid_tendency(ensemble[0], mixing)
+    modal_grid = mix_levels(to_modes, grid_rounded).astype(jnp.bfloat16)
+    outgoing = pl.pallas_call(
+        spread_kernel,
+        out_shape=jax.ShapeDtypeStruct(
+            (local_waves, quarters, 2 * lat_count, lanes), jnp.bfloat16
+        ),
+        in_specs=[smem, vmem, vmem, vmem],
+        out_specs=vmem,
+        name="spread_fourier",
+    )(
+        counts.astype(jnp.float32),
+        pair_forward.T,
+        modal_grid.reshape(level_count * row_count, longitudes),
+        lane_scale,
+    )
+    everyone = ("traj", "lat")
+    arrived = lax.all_to_all(
+        outgoing.reshape(traj_count * lat_count, 2, lanes), everyone, 0, 0, tiled=True
+    )
+    arrived = arrived.reshape(traj_count, lat_count, 2, lanes).transpose(1, 0, 2, 3)
+    band_parts = pl.pallas_call(
+        wave_kernel,
+        out_shape=jax.ShapeDtypeStruct((lat_count, 2 * traj_count, lanes), jnp.bfloat16),
+        in_specs=[vmem, vmem, vmem, vmem],
+        out_specs=vmem,
+        scratch_shapes=[
+            pltpu.VMEM((modes, lat_count * row_count, 2 * traj_count), jnp.float32),
+            pltpu.VMEM((lat_count, used, 2 * traj_count), jnp.float32),
+        ],
+        name="wave_solve",
+    )(
+        arrived.reshape(lat_count, 2 * traj_count, lanes),
+        own_table,
+        own_table.T,
+        own_inverse,
+    )
+    band_parts = band_parts.reshape(lat_count, traj_count, 2, lanes).transpose(1, 0, 2, 3)
+    returned = lax.all_to_all(
+        band_parts.reshape(traj_count * lat_count, 2, lanes), everyone, 0, 0, tiled=True
+    )
+    returned = returned.reshape(local_waves, quarters, 2 * lat_count, lanes).transpose(1, 0, 2, 3)
+    modal_grid = pl.pallas_call(
+        gather_kernel,
+        out_shape=jax.ShapeDtypeStruct((level_count * row_count, longitudes), jnp.bfloat16),
+        in_specs=[vmem, vmem],
+        out_specs=vmem,
+        name="gather_fourier",
+    )(returned.reshape(quarters, 2 * total_waves, lanes), pair_backward)
+    state_grid = mix_levels(from_modes, modal_grid.reshape(level_count, row_count, longitudes))
     state_grid = to_band_grid(to_implicit(grid_section(state_grid, mixing, lat_scale, forward)))
     return state_grid[None]
 

time: 321 us -> 268 us (0.83)
  the two profiles are of different devices: /device:TPU:34 before, /device:TPU:32 now
where the time goes in v1:
time: 268 us; the launch traced here: 267 us
  waiting for transfers between devices  160 us (60%)
  starting transfers between devices  40.8 us (15%)
  local copies, waits for them, and re-layouts  36.4 us (14%)
  matrix products  11.2 us (4%)
  Pallas kernels  11 us (4%)
  other arithmetic  6.35 us (2%)
    all_to_all x1, waiting for transfers between devices, local(): lax.all_to_all(band_parts.reshape(traj_count * lat_count, 2, lanes), ever...  47.1 us
    all_to_all x1, waiting for transfers between devices, local(): lax.all_to_all(outgoing.reshape(traj_count * lat_count, 2, lanes), everyo...  44.9 us
    all_to_all x1, waiting for transfers between devices, to_implicit(): lax.all_to_all(coefficients, 'lat', split_axis=2, concat_axis=1, tiled=True)  36.3 us
    all_to_all x1, waiting for transfers between devices, to_band_grid(): lax.all_to_all(band_parts, 'lat', split_axis=1, concat_axis=2, tiled=True)  31.9 us
    all_to_all x1, starting transfers between devices, local(): lax.all_to_all(outgoing.reshape(traj_count * lat_count, 2, lanes), everyo...  23 us
    unnamed x16, local copies, waits for them, and re-layouts  13.4 us
    all_to_all x1, starting transfers between devices, local(): lax.all_to_all(band_parts.reshape(traj_count * lat_count, 2, lanes), ever...  9.18 us
    pallas_call x1, Pallas kernels, local(): pl.pallas_call(wave_kernel, out_shape=jax.ShapeDtypeStruct((lat_count, 2...  5.49 us
  transfers between devices with their start and end apart: 4, of which 4 were waited for; matrix products, arithmetic and copies ran while one was open for 1% of the time, Pallas kernels for 0%

profile of v1, /device:TPU:32, one launch (start us, length us, event | category | flops | bytes accessed | tf_op | source)
XLA Modules:
  0.0 267.2 jit_solution(2238124197556535466)
XLA Ops:
  0.8 0.7 broadcast_multiply_fusion
  1.6 0.6 broadcast_in_dim.43.scale_ref
  2.2 1.7 convert_element_type.84
  3.9 0.9 fusion.12
  4.9 0.6 copy-done.3
  5.6 0.4 fusion
  6.0 1.4 convert_element_type.90.grid_ref
  7.4 2.6 multiply_convert_fusion.1
  10.1 2.8 %spread_fourier.1 = bf16[16,4,16,384]{3,2,1,0:T(8,128)(2,1)} custom-call(f32[1]{0:T(128)S(6)} %convert_element_type.81.count_ref, bf16[256,384]{1,0:T(8,128)(2,1)} %get-tuple-element.6.table_ref, bf16[1344,384]{1,0:T(8,128)(2,1)} %convert_element_type.90.grid_ref, f32[1,384]{1,0:T(1,128)} %broadcast_in_dim.43.scale_ref), custom_call_target="tpu_custom_call" | custom-call | tf_op jit(solution)/shard_map/spread_fourier/pallas_call | solution.py:214
  12.9 2.9 %reshape.207 = bf16[512,2,384]{2,1,0:T(2,128)(2,1)} reshape(bf16[16,4,16,384]{3,2,1,0:T(8,128)(2,1)} %spread_fourier.1) | data formatting | bytes 1572864 | tf_op jit(solution)/shard_map/reshape | solution.py:230
  15.7 23.0 %all-to-all-start = ((bf16[512,2,384]{2,1,0:T(2,128)(2,1)}), bf16[512,2,384]{2,1,0:T(2,128)(2,1)S(1)}, u32[]{:S(2)}, u32[]{:S(2)}) async-start(bf16[512,2,384]{2,1,0:T(2,128)(2,1)} %reshape.207), calls=%async_computation | async-start | bytes 1572864 | tf_op jit(solution)/shard_map/all_to_all | solution.py:229
  38.8 0.7 copy.95
  39.6 0.6 fusion.91.table_ref
  40.3 0.7 divide_bitcast_fusion.inverse_ref
  41.0 44.9 %all-to-all-done = bf16[512,2,384]{2,1,0:T(2,128)(2,1)S(1)} async-done(((bf16[512,2,384]{2,1,0:T(2,128)(2,1)}), bf16[512,2,384]{2,1,0:T(2,128)(2,1)S(1)}, u32[]{:S(2)}, u32[]{:S(2)}) %all-to-all-start) | async-done | bytes 786464 | tf_op jit(solution)/shard_map/all_to_all | solution.py:229
  86.0 0.8 copy.94
  86.9 1.2 reshape.209.parts_ref
  88.0 5.5 %wave_solve.1 = bf16[8,128,384]{2,1,0:T(8,128)(2,1)} custom-call(bf16[8,128,384]{2,1,0:T(8,128)(2,1)} %reshape.209.parts_ref, bf16[192,128]{1,0:T(8,128)(2,1)} %fusion.91.table_ref, bf16[128,192]{1,0:T(8,128)(2,1)} %bitcast.130, f32[128,14]{1,0:T(8,128)} %divide_bitcast_fusion.inverse_ref), custom_call_target="tpu_custom_call" | custom-call | tf_op jit(solution)/shard_map/wave_solve/pallas_call | solution.py:233
  93.5 2.2 reshape.210
  95.7 0.5 copy.151
  96.1 1.7 copy.99
  97.8 9.2 %all-to-all-start.1 = ((bf16[512,2,384]{2,1,0:T(2,128)(2,1)}), bf16[512,2,384]{2,1,0:T(2,128)(2,1)S(1)}, u32[]{:S(2)}, u32[]{:S(2)}) async-start(bf16[512,2,384]{2,1,0:T(2,128)(2,1)} %copy.99), calls=%async_computation.1 | async-start | bytes 1572864 | tf_op jit(solution)/shard_map/all_to_all | solution.py:250
  107.0 47.1 %all-to-all-done.1 = bf16[512,2,384]{2,1,0:T(2,128)(2,1)S(1)} async-done(((bf16[512,2,384]{2,1,0:T(2,128)(2,1)}), bf16[512,2,384]{2,1,0:T(2,128)(2,1)S(1)}, u32[]{:S(2)}, u32[]{:S(2)}) %all-to-all-start.1) | async-done | bytes 786464 | tf_op jit(solution)/shard_map/all_to_all | solution.py:250
  154.5 1.0 copy.100
  155.5 2.7 %gather_fourier.1 = bf16[1344,384]{1,0:T(8,128)(2,1)} custom-call(bf16[4,256,384]{2,1,0:T(8,128)(2,1)} %bitcast.128, bf16[256,384]{1,0:T(8,128)(2,1)} %get-tuple-element.5.table_ref), custom_call_target="tpu_custom_call" | custom-call | tf_op jit(solution)/shard_map/gather_fourier/pallas_call | solution.py:254
  158.2 1.6 reshape_reshape.3
  159.8 0.4 fusion.61
  160.2 0.4 fusion.82
  160.6 0.5 fusion.8
  161.1 2.1 fusion.11
  163.2 1.1 copy.107
  164.4 3.5 %reshape.225 = bf16[8,2,21504]{2,1,0:T(2,128)(2,1)} reshape(bf16[256,24,56]{2,1,0:T(8,128)(2,1)S(1)} %bitcast.117) | data formatting | bytes 1376256
  167.9 3.8 %all-to-all-start.2 = ((bf16[8,2,21504]{2,1,0:T(2,128)(2,1)}), bf16[8,2,21504]{2,1,0:T(2,128)(2,1)S(1)}, u32[]{:S(2)}, u32[]{:S(2)}) async-start(bf16[8,2,21504]{2,1,0:T(2,128)(2,1)} %reshape.225), calls=%async_computation.2 | async-start | bytes 1376256 | tf_op jit(solution)/shard_map/all_to_all | solution.py:186
  171.8 36.3 %all-to-all-done.2 = bf16[8,2,21504]{2,1,0:T(2,128)(2,1)S(1)} async-done(((bf16[8,2,21504]{2,1,0:T(2,128)(2,1)}), bf16[8,2,21504]{2,1,0:T(2,128)(2,1)S(1)}, u32[]{:S(2)}, u32[]{:S(2)}) %all-to-all-start.2) | async-done | bytes 688160 | tf_op jit(solution)/shard_map/all_to_all | solution.py:186
  208.1 2.8 %reshape.226 = bf16[256,24,56]{2,1,0:T(8,128)(2,1)S(1)} reshape(bf16[8,2,21504]{2,1,0:T(2,128)(2,1)S(1)} %all-to-all-done.2) | data formatting | bytes 1376256
  210.9 0.3 copy.109
  211.2 0.9 fusion.13
  212.2 1.0 fusion.17
  213.1 1.0 fusion.18
  214.1 0.6 fusion.16
  215.1 2.1 copy.115
  217.2 3.5 %reshape.227 = bf16[8,2,21504]{2,1,0:T(2,128)(2,1)} reshape(bf16[192,32,56]{2,1,0:T(8,128)(2,1)S(1)} %bitcast.120) | data formatting | bytes 1376256
  220.7 4.8 %all-to-all-start.3 = ((bf16[8,2,21504]{2,1,0:T(2,128)(2,1)}), bf16[8,2,21504]{2,1,0:T(2,128)(2,1)S(1)}, u32[]{:S(2)}, u32[]{:S(2)}) async-start(bf16[8,2,21504]{2,1,0:T(2,128)(2,1)} %reshape.227), calls=%async_computation.3 | async-start | bytes 1376256 | tf_op jit(solution)/shard_map/all_to_all | solution.py:196
  225.5 31.9 %all-to-all-done.3 = bf16[8,2,21504]{2,1,0:T(2,128)(2,1)S(1)} async-done(((bf16[8,2,21504]{2,1,0:T(2,128)(2,1)}), bf16[8,2,21504]{2,1,0:T(2,128)(2,1)S(1)}, u32[]{:S(2)}, u32[]{:S(2)}) %all-to-all-start.3) | async-done | bytes 688160 | tf_op jit(solution)/shard_map/all_to_all | solution.py:196
  257.4 2.8 %reshape.228 = bf16[192,32,56]{2,1,0:T(8,128)(2,1)S(1)} reshape(bf16[8,2,21504]{2,1,0:T(2,128)(2,1)S(1)} %all-to-all-done.3) | data formatting | bytes 1376256
  260.2 1.6 copy.116
  261.8 1.8 copy.117
  263.7 3.5 %convolution_bitcast_fusion = f32[1,56,24,384]{3,2,1,0:T(8,128)} fusion(bf16[56,24,256]{2,1,0:T(8,128)(2,1)S(1)} %copy.117, s32[256]{0:T(256)S(1)} %fusion.67, f32[256]{0:T(256)S(1)} %compare_select_fusion.2, pred[256]{0:T(512)(128)(4,1)S(1)} %fusion.73), kind=kOutput, calls=%fused_computation.13 | convolution fusion | flops 265519104 | bytes 2754816 | tf_op jit(solution)/shard_map/dot_general | solution.py:181
  (28 shorter events, 1.1 us)
Async XLA Ops:
  0.0 38.8 %copy-start = (bf16[16,192,128]{2,1,0:T(8,128)(2,1)S(1)}, bf16[16,192,128]{2,1,0:T(8,128)(2,1)}, u32[]{:S(2)}) copy-start(bf16[16,192,128]{2,1,0:T(8,128)(2,1)} %param.12) | copy-start | bytes 2359300
  0.0 3.9 %copy-start.1 = (f32[1,56,24,384]{3,2,1,0:T(8,128)S(1)}, f32[1,56,24,384]{3,2,1,0:T(8,128)}, u32[]{:S(2)}) copy-start(f32[1,56,24,384]{3,2,1,0:T(8,128)} %param.8) | copy-start | bytes 6193156
  0.0 3.9 %copy-start.4 = (bf16[56,56]{1,0:T(8,128)(2,1)S(1)}, bf16[56,56]{1,0:T(8,128)(2,1)}, u32[]{:S(2)}) copy-start(bf16[56,56]{1,0:T(8,128)(2,1)} %param.10) | copy-start | bytes 18820
  4.8 0.8 copy-start.3
  12.9 27.3 %copy-start.5 = (f32[56]{0:T(128)S(1)}, f32[56]{0:T(128)}, u32[]{:S(2)}) copy-start(f32[56]{0:T(128)} %param.15) | copy-start | bytes 676
  15.7 70.2 %all-to-all-start = ((bf16[512,2,384]{2,1,0:T(2,128)(2,1)}), bf16[512,2,384]{2,1,0:T(2,128)(2,1)S(1)}, u32[]{:S(2)}, u32[]{:S(2)}) async-start(bf16[512,2,384]{2,1,0:T(2,128)(2,1)} %reshape.207), calls=%async_computation | async-start | bytes 1572864 | tf_op jit(solution)/shard_map/all_to_all | solution.py:229
  97.8 56.3 %all-to-all-start.1 = ((bf16[512,2,384]{2,1,0:T(2,128)(2,1)}), bf16[512,2,384]{2,1,0:T(2,128)(2,1)S(1)}, u32[]{:S(2)}, u32[]{:S(2)}) async-start(bf16[512,2,384]{2,1,0:T(2,128)(2,1)} %copy.99), calls=%async_computation.1 | async-start | bytes 1572864 | tf_op jit(solution)/shard_map/all_to_all | solution.py:250
  155.5 4.3 %copy-start.2 = (f32[56,56]{1,0:T(8,128)S(1)}, f32[56,56]{1,0:T(8,128)}, u32[]{:S(2)}) copy-start(f32[56,56]{1,0:T(8,128)} %param.14) | copy-start | bytes 37636
  167.9 40.2 %all-to-all-start.2 = ((bf16[8,2,21504]{2,1,0:T(2,128)(2,1)}), bf16[8,2,21504]{2,1,0:T(2,128)(2,1)S(1)}, u32[]{:S(2)}, u32[]{:S(2)}) async-start(bf16[8,2,21504]{2,1,0:T(2,128)(2,1)} %reshape.225), calls=%async_computation.2 | async-start | bytes 1376256 | tf_op jit(solution)/shard_map/all_to_all | solution.py:186
  220.7 36.7 %all-to-all-start.3 = ((bf16[8,2,21504]{2,1,0:T(2,128)(2,1)}), bf16[8,2,21504]{2,1,0:T(2,128)(2,1)S(1)}, u32[]{:S(2)}, u32[]{:S(2)}) async-start(bf16[8,2,21504]{2,1,0:T(2,128)(2,1)} %reshape.227), calls=%async_computation.3 | async-start | bytes 1376256 | tf_op jit(solution)/shard_map/all_to_all | solution.py:196

commit v2 on v1

--- a/solution.py
+++ b/solution.py
@@ -2,6 +2,7 @@
 
 import jax
 import jax.numpy as jnp
+import numpy as np
 from jax import lax
 from jax.experimental import pallas as pl
 from jax.experimental.pallas import tpu as pltpu
@@ -12,12 +13,13 @@
 
 
 def fourier_tables(wavenumber, component, longitudes):
-    positions = jnp.arange(longitudes, dtype=jnp.int32)
+    positions = np.arange(longitudes)
     product_index = positions[:, None] * wavenumber[None, :] % longitudes
-    angles = 2.0 * math.pi / longitudes * product_index.astype(jnp.float32)
-    signed = jnp.where(component[None, :] == 0, jnp.cos(angles), -jnp.sin(angles))
-    factor = jnp.where(wavenumber == 0, 1.0, 2.0).astype(jnp.float32)
-    return (signed.astype(jnp.bfloat16), (factor[None, :] * signed).T.astype(jnp.bfloat16))
+    angles = 2.0 * math.pi / longitudes * product_index
+    signed = np.where(component[None, :] == 0, np.cos(angles), -np.sin(angles))
+    factor = np.where(wavenumber == 0, 1.0, 2.0)
+    rounded = jnp.bfloat16
+    return signed.astype(rounded), (factor[None, :] * signed).T.astype(rounded)
 
 
 def mode_divisor(mode_rates, degree_count):
@@ -67,19 +69,19 @@
     return test(row, col)
 
 
-def spread_kernel(count_ref, table_ref, grid_ref, scale_ref, out_ref):
-    wave_count, quarters, pair_rows, lanes = out_ref.shape
+def spread_kernel(count_ref, table_ref, grid_ref, out_ref):
+    wave_count, quarters, lat_count, _, lanes = out_ref.shape
     used = grid_ref.shape[0] // quarters
     table = table_ref[...]
-    lane = lax.broadcasted_iota(jnp.int32, (wave_count * pair_rows, lanes), 1)
+    lane = lax.broadcasted_iota(jnp.int32, table.shape[:1] + (lanes,), 1)
     for quarter in range(quarters):
         block = grid_ref[quarter * used : (quarter + 1) * used, :]
         block = jnp.concatenate(
             [block, jnp.zeros((lanes - used, block.shape[1]), block.dtype)], axis=0
         )
-        sums = contract(table, block, 1, 1) * scale_ref[...]
+        sums = contract(table, block, 1, 1)
         sums = jnp.where(lane < used, sums, count_ref[0])
-        out_ref[:, quarter] = sums.astype(jnp.bfloat16).reshape(wave_count, pair_rows, lanes)
+        out_ref[:, quarter] = sums.astype(jnp.bfloat16).reshape(wave_count, lat_count, 2, lanes)
 
 
 def selection(count_row, size):
@@ -109,14 +111,15 @@
 
 
 def wave_kernel(parts_ref, table_ref, turned_ref, inverse_ref, out_ref, wave_ref, band_ref):
-    lat_count, size, lanes = parts_ref.shape
+    members, lat_count, _, lanes = parts_ref.shape
+    size = 2 * members
     modes, lat_rows, _ = wave_ref.shape
     rows = lat_rows // lat_count
     used = modes * rows
     unit = jnp.where(block_mask(used + 8, lanes, lambda r, c: r == c), 1.0, 0.0).astype(jnp.bfloat16)
     pick = None
     for lat in range(lat_count):
-        turned = contract(unit, parts_ref[lat], 1, 1)
+        turned = contract(unit, parts_ref[:, lat].reshape(size, lanes), 1, 1)
         if lat == 0:
             pick = selection(turned[used : used + 8], size)
         for mode in range(modes):
@@ -129,17 +132,20 @@
         band = contract(table, modal, 1, 0)
         for lat in range(lat_count):
             band_ref[lat, mode * rows : (mode + 1) * rows, :] = band[lat * rows : (lat + 1) * rows]
-    out_ref[...] = jnp.zeros(out_ref.shape, out_ref.dtype)
+    spare = jnp.zeros((lanes - used, band_ref.shape[2]), jnp.bfloat16)
     for lat in range(lat_count):
-        chosen = contract(pick, band_ref[lat].astype(jnp.bfloat16), 1, 1)
-        out_ref[lat, :, 0:used] = chosen.astype(jnp.bfloat16)
+        band = jnp.concatenate([band_ref[lat].astype(jnp.bfloat16), spare], axis=0)
+        chosen = contract(pick, band, 1, 1).astype(jnp.bfloat16)
+        out_ref[:, lat] = chosen.reshape(members, 2, lanes)
 
 
 def gather_kernel(parts_ref, table_ref, out_ref):
-    quarters = parts_ref.shape[0]
+    _, quarters, _, _, lanes = parts_ref.shape
     used = out_ref.shape[0] // quarters
     for quarter in range(quarters):
-        sums = contract(parts_ref[quarter], table_ref[...], 0, 0)
+        sums = contract(
+            parts_ref[:, quarter].reshape(table_ref.shape[0], lanes), table_ref[...], 0, 0
+        )
         out_ref[quarter * used : (quarter + 1) * used, :] = sums[:used].astype(jnp.bfloat16)
 
 
@@ -160,7 +166,7 @@
     degree_count = legendre.shape[2]
     total_waves = local_waves * lat_count
     longitudes = ensemble.shape[3]
-    columns = jnp.arange(2 * total_waves, dtype=jnp.int32)
+    columns = np.arange(2 * total_waves)
     within = columns % (2 * local_waves)
     wavenumber = columns // (2 * local_waves) * local_waves + within % local_waves
     component = within // local_waves
@@ -200,39 +206,37 @@
     modes = level_count // quarters
     used = modes * row_count
     lanes = -(-(used + 1) // 128) * 128
-    pairs = jnp.arange(2 * total_waves, dtype=jnp.int32)
+    pairs = np.arange(2 * total_waves)
     pair_wave = pairs // 2 % lat_count * local_waves + pairs // (2 * lat_count)
     pair_forward, pair_backward = fourier_tables(pair_wave, pairs % 2, longitudes)
     traj_index = lax.axis_index("traj")
     own_table = lax.dynamic_index_in_dim(legendre, traj_index // quarters, 0, keepdims=False)
     own_divisor = lax.dynamic_slice_in_dim(divisor, traj_index % quarters * modes, modes, 0)
     own_inverse = (1.0 / own_divisor).T
-    lane_scale = jnp.pad(jnp.tile(lat_scale, modes), (0, lanes - used))[None, :]
 
     grid_rounded = grid_tendency(ensemble[0], mixing)
-    modal_grid = mix_levels(to_modes, grid_rounded).astype(jnp.bfloat16)
+    modal_grid = mix_levels(to_modes, grid_rounded) * lat_scale[None, :, None]
+    modal_grid = modal_grid.astype(jnp.bfloat16)
     outgoing = pl.pallas_call(
         spread_kernel,
         out_shape=jax.ShapeDtypeStruct(
-            (local_waves, quarters, 2 * lat_count, lanes), jnp.bfloat16
+            (local_waves, quarters, lat_count, 2, lanes), jnp.bfloat16
         ),
-        in_specs=[smem, vmem, vmem, vmem],
+        in_specs=[smem, vmem, vmem],
         out_specs=vmem,
         name="spread_fourier",
     )(
         counts.astype(jnp.float32),
-        pair_forward.T,
+        np.ascontiguousarray(pair_forward.T),
         modal_grid.reshape(level_count * row_count, longitudes),
-        lane_scale,
     )
     everyone = ("traj", "lat")
     arrived = lax.all_to_all(
         outgoing.reshape(traj_count * lat_count, 2, lanes), everyone, 0, 0, tiled=True
     )
-    arrived = arrived.reshape(traj_count, lat_count, 2, lanes).transpose(1, 0, 2, 3)
     band_parts = pl.pallas_call(
         wave_kernel,
-        out_shape=jax.ShapeDtypeStruct((lat_count, 2 * traj_count, lanes), jnp.bfloat16),
+        out_shape=jax.ShapeDtypeStruct((traj_count, lat_count, 2, lanes), jnp.bfloat16),
         in_specs=[vmem, vmem, vmem, vmem],
         out_specs=vmem,
         scratch_shapes=[
@@ -241,23 +245,21 @@
         ],
         name="wave_solve",
     )(
-        arrived.reshape(lat_count, 2 * traj_count, lanes),
+        arrived.reshape(traj_count, lat_count, 2, lanes),
         own_table,
         own_table.T,
         own_inverse,
     )
-    band_parts = band_parts.reshape(lat_count, traj_count, 2, lanes).transpose(1, 0, 2, 3)
     returned = lax.all_to_all(
         band_parts.reshape(traj_count * lat_count, 2, lanes), everyone, 0, 0, tiled=True
     )
-    returned = returned.reshape(local_waves, quarters, 2 * lat_count, lanes).transpose(1, 0, 2, 3)
     modal_grid = pl.pallas_call(
         gather_kernel,
         out_shape=jax.ShapeDtypeStruct((level_count * row_count, longitudes), jnp.bfloat16),
         in_specs=[vmem, vmem],
         out_specs=vmem,
         name="gather_fourier",
-    )(returned.reshape(quarters, 2 * total_waves, lanes), pair_backward)
+    )(returned.reshape(local_waves, quarters, lat_count, 2, lanes), pair_backward)
     state_grid = mix_levels(from_modes, modal_grid.reshape(level_count, row_count, longitudes))
     state_grid = to_band_grid(to_implicit(grid_section(state_grid, mixing, lat_scale, forward)))
     return state_grid[None]

time: 268 us -> 257 us (0.959)
  the two profiles are of different devices: /device:TPU:32 before, /device:TPU:34 now
where the time goes in v2:
time: 257 us; the launch traced here: 256 us
  blocking collectives  92.6 us (36%)
  waiting for transfers between devices  83.8 us (33%)
  local copies, waits for them, and re-layouts  27.1 us (11%)
  starting transfers between devices  26.6 us (10%)
  Pallas kernels  11.2 us (4%)
  matrix products  9.25 us (4%)
  other arithmetic  4.9 us (2%)
    all_to_all x1, blocking collectives, local(): lax.all_to_all(band_parts.reshape(traj_count * lat_count, 2, lanes), ever...  58 us
    all_to_all x1, waiting for transfers between devices, local(): lax.all_to_all(outgoing.reshape(traj_count * lat_count, 2, lanes), everyo...  44 us
    all_to_all x1, waiting for transfers between devices, to_implicit(): lax.all_to_all(coefficients, 'lat', split_axis=2, concat_axis=1, tiled=True)  39.8 us
    all_to_all x1, blocking collectives, to_band_grid(): lax.all_to_all(band_parts, 'lat', split_axis=1, concat_axis=2, tiled=True)  34.6 us
    all_to_all x1, starting transfers between devices, local(): lax.all_to_all(outgoing.reshape(traj_count * lat_count, 2, lanes), everyo...  23 us
    unnamed x22, local copies, waits for them, and re-layouts  14.9 us
    pallas_call x1, Pallas kernels, local(): pl.pallas_call(wave_kernel, out_shape=jax.ShapeDtypeStruct((traj_count, l...  5.49 us
  transfers between devices with their start and end apart: 2, of which 2 were waited for; matrix products, arithmetic and copies ran while one was open for 1% of the time, Pallas kernels for 0%

profile of v2, /device:TPU:34, one launch (start us, length us, event | category | flops | bytes accessed | tf_op | source)
XLA Modules:
  0.0 256.5 jit_solution(988580852209797508)
XLA Ops:
  0.8 0.7 broadcast_multiply_fusion
  1.5 0.1 mul.85
  1.6 1.7 convert_element_type.48
  3.3 0.9 fusion.11
  4.2 0.0 copy-start.5
  4.2 0.1 copy.109
  4.3 0.6 copy-done.5
  5.0 1.7 convolution_bitcast_fusion
  6.7 1.7 reshape.91
  8.4 1.2 multiply_convert_fusion.grid_ref
  9.6 2.9 %spread_fourier.1 = bf16[16,4,8,2,384]{4,3,2,1,0:T(2,128)(2,1)} custom-call(f32[1]{0:T(128)S(6)} %convert_element_type.47.count_ref, bf16[256,384]{1,0:T(8,128)(2,1)} %constant.64.clone.table_ref, bf16[1344,384]{1,0:T(8,128)(2,1)} %multiply_convert_fusion.grid_ref), custom_call_target="tpu_custom_call" | custom-call | tf_op jit(solution)/shard_map/spread_fourier/pallas_call | solution.py:220
  12.5 23.0 %all-to-all-start = ((bf16[512,2,384]{2,1,0:T(2,128)(2,1)}), bf16[512,2,384]{2,1,0:T(2,128)(2,1)S(1)}, u32[]{:S(2)}, u32[]{:S(2)}) async-start(bf16[512,2,384]{2,1,0:T(2,128)(2,1)} %bitcast.114), calls=%async_computation | async-start | bytes 1572864 | tf_op jit(solution)/shard_map/all_to_all | solution.py:234
  35.6 0.7 copy.82
  36.3 0.6 fusion.45.table_ref
  36.9 0.1 multiply_add_fusion
  37.0 0.7 divide_bitcast_fusion.inverse_ref
  37.8 44.0 %all-to-all-done = bf16[512,2,384]{2,1,0:T(2,128)(2,1)S(1)} async-done(((bf16[512,2,384]{2,1,0:T(2,128)(2,1)}), bf16[512,2,384]{2,1,0:T(2,128)(2,1)S(1)}, u32[]{:S(2)}, u32[]{:S(2)}) %all-to-all-start) | async-done | bytes 786464 | tf_op jit(solution)/shard_map/all_to_all | solution.py:234
  81.8 0.9 copy-done.1
  82.7 5.5 %wave_solve.1 = bf16[64,8,2,384]{3,2,1,0:T(2,128)(2,1)} custom-call(bf16[64,8,2,384]{3,2,1,0:T(2,128)(2,1)} %bitcast.113, bf16[192,128]{1,0:T(8,128)(2,1)} %fusion.45.table_ref, bf16[128,192]{1,0:T(8,128)(2,1)} %bitcast.118, f32[128,14]{1,0:T(8,128)} %divide_bitcast_fusion.inverse_ref), custom_call_target="tpu_custom_call" | custom-call | tf_op jit(solution)/shard_map/wave_solve/pallas_call | solution.py:237
  88.2 58.0 %all_to_all.40 = bf16[512,2,384]{2,1,0:T(2,128)(2,1)} all-to-all(bf16[512,2,384]{2,1,0:T(2,128)(2,1)} %bitcast.115), channel_id=1, replica_groups=mesh['traj'=64,'lat'=8] {'traj','lat'}, dimensions={0} | all-to-all | bytes 1572864 | tf_op jit(solution)/shard_map/all_to_all | solution.py:253
  146.2 2.8 %gather_fourier.1 = bf16[1344,384]{1,0:T(8,128)(2,1)} custom-call(bf16[16,4,8,2,384]{4,3,2,1,0:T(2,128)(2,1)} %bitcast.116, bf16[256,384]{1,0:T(8,128)(2,1)} %constant.65.clone.table_ref), custom_call_target="tpu_custom_call" | custom-call | tf_op jit(solution)/shard_map/gather_fourier/pallas_call | solution.py:256
  148.9 1.6 reshape_reshape.3
  150.6 0.4 fusion.29
  151.0 0.4 fusion.34
  151.4 0.0 copy-start.8
  151.4 0.5 fusion.7
  151.9 0.4 copy-done.8
  152.3 0.5 fusion.10
  152.8 1.1 copy.91
  154.0 3.5 %reshape.107 = bf16[8,2,21504]{2,1,0:T(2,128)(2,1)} reshape(bf16[256,24,56]{2,1,0:T(8,128)(2,1)S(1)} %bitcast.105) | data formatting | bytes 1376256
  157.5 3.5 %all-to-all-start.2 = ((bf16[8,2,21504]{2,1,0:T(2,128)(2,1)}), bf16[8,2,21504]{2,1,0:T(2,128)(2,1)S(1)}, u32[]{:S(2)}, u32[]{:S(2)}) async-start(bf16[8,2,21504]{2,1,0:T(2,128)(2,1)} %reshape.107), calls=%async_computation.2 | async-start | bytes 1376256 | tf_op jit(solution)/shard_map/all_to_all | solution.py:192
  161.1 0.1 copy.96
  161.1 39.8 %all-to-all-done.2 = bf16[8,2,21504]{2,1,0:T(2,128)(2,1)S(1)} async-done(((bf16[8,2,21504]{2,1,0:T(2,128)(2,1)}), bf16[8,2,21504]{2,1,0:T(2,128)(2,1)S(1)}, u32[]{:S(2)}, u32[]{:S(2)}) %all-to-all-start.2) | async-done | bytes 688160 | tf_op jit(solution)/shard_map/all_to_all | solution.py:192
  201.0 2.8 %reshape.108 = bf16[256,24,56]{2,1,0:T(8,128)(2,1)S(1)} reshape(bf16[8,2,21504]{2,1,0:T(2,128)(2,1)S(1)} %all-to-all-done.2) | data formatting | bytes 1376256
  203.8 0.3 copy.93
  204.1 0.9 fusion.12
  205.0 1.0 fusion.16
  206.0 1.0 fusion.17
  207.0 0.6 fusion.15
  207.6 0.3 copy.98
  207.9 2.1 copy.99
  210.0 2.8 %reshape.109 = bf16[8,2,21504]{2,1,0:T(2,128)(2,1)S(1)} reshape(bf16[192,32,56]{2,1,0:T(8,128)(2,1)S(1)} %bitcast.108) | data formatting | bytes 1376256
  212.8 34.6 %all_to_all.41 = bf16[8,2,21504]{2,1,0:T(2,128)(2,1)} all-to-all(bf16[8,2,21504]{2,1,0:T(2,128)(2,1)S(1)} %reshape.109), channel_id=1, replica_groups=mesh['traj'=64,'lat'=8] {'lat'}, dimensions={0} | all-to-all | bytes 1376256 | tf_op jit(solution)/shard_map/all_to_all | solution.py:202
  247.4 3.8 %reshape.110 = bf16[192,32,56]{2,1,0:T(8,128)(2,1)S(1)} reshape(bf16[8,2,21504]{2,1,0:T(2,128)(2,1)} %all_to_all.41) | data formatting | bytes 1376256
  251.2 0.0 copy-start.3
  251.2 1.6 copy.100
  252.8 1.8 copy.101
  254.6 1.8 convolution_bitcast_fusion.1
  (15 shorter events, 0.0 us)
Async XLA Ops:
  0.0 35.5 %copy-start = (bf16[16,192,128]{2,1,0:T(8,128)(2,1)S(1)}, bf16[16,192,128]{2,1,0:T(8,128)(2,1)}, u32[]{:S(2)}) copy-start(bf16[16,192,128]{2,1,0:T(8,128)(2,1)} %param.16) | copy-start | bytes 2359300
  0.0 3.3 %copy-start.2 = (f32[1,56,24,384]{3,2,1,0:T(8,128)S(1)}, f32[1,56,24,384]{3,2,1,0:T(8,128)}, u32[]{:S(2)}) copy-start(f32[1,56,24,384]{3,2,1,0:T(8,128)} %param.12) | copy-start | bytes 6193156
  0.0 3.3 %copy-start.6 = (bf16[56,56]{1,0:T(8,128)(2,1)S(1)}, bf16[56,56]{1,0:T(8,128)(2,1)}, u32[]{:S(2)}) copy-start(bf16[56,56]{1,0:T(8,128)(2,1)} %param.14) | copy-start | bytes 18820
  4.2 0.8 copy-start.5
  9.6 27.4 %copy-start.7 = (f32[56]{0:T(128)S(1)}, f32[56]{0:T(128)}, u32[]{:S(2)}) copy-start(f32[56]{0:T(128)} %param.19) | copy-start | bytes 676
  12.5 69.3 %all-to-all-start = ((bf16[512,2,384]{2,1,0:T(2,128)(2,1)}), bf16[512,2,384]{2,1,0:T(2,128)(2,1)S(1)}, u32[]{:S(2)}, u32[]{:S(2)}) async-start(bf16[512,2,384]{2,1,0:T(2,128)(2,1)} %bitcast.114), calls=%async_computation | async-start | bytes 1572864 | tf_op jit(solution)/shard_map/all_to_all | solution.py:234
  81.8 0.9 copy-start.1
  146.2 4.3 %copy-start.4 = (f32[56,56]{1,0:T(8,128)S(1)}, f32[56,56]{1,0:T(8,128)}, u32[]{:S(2)}) copy-start(f32[56,56]{1,0:T(8,128)} %param.18) | copy-start | bytes 37636
  151.4 0.9 copy-start.8
  157.5 43.4 %all-to-all-start.2 = ((bf16[8,2,21504]{2,1,0:T(2,128)(2,1)}), bf16[8,2,21504]{2,1,0:T(2,128)(2,1)S(1)}, u32[]{:S(2)}, u32[]{:S(2)}) async-start(bf16[8,2,21504]{2,1,0:T(2,128)(2,1)} %reshape.107), calls=%async_computation.2 | async-start | bytes 1376256 | tf_op jit(solution)/shard_map/all_to_all | solution.py:192
  251.2 3.5 %copy-start.3 = (bf16[256,384,1]{1,0,2:T(8,128)(2,1)S(1)}, bf16[256,384,1]{1,0,2:T(8,128)(2,1)}, u32[]{:S(2)}) copy-start(bf16[256,384,1]{1,0,2:T(8,128)(2,1)} %constant.71) | copy-start | bytes 589828

commit v3 on v2

--- a/solution.py
+++ b/solution.py
@@ -69,19 +69,29 @@
     return test(row, col)
 
 
-def spread_kernel(count_ref, table_ref, grid_ref, out_ref):
+def first_kernel(
+    count_ref, weight_ref, table_ref, mixing_ref, to_ref, grid_ref, out_ref, modal_ref
+):
+    level_count, row_count, longitudes = grid_ref.shape
     wave_count, quarters, lat_count, _, lanes = out_ref.shape
-    used = grid_ref.shape[0] // quarters
+    modes = level_count // quarters
+    used = modes * row_count
+    mixing, to_modes = mixing_ref[...], to_ref[...]
+    for row in range(row_count):
+        state = grid_ref[:, row, :]
+        mixed = contract(mixing, state.astype(jnp.bfloat16), 1, 0)
+        tendency = state + time_step * (mixed - cubic_rate * state * state * state)
+        modal = contract(to_modes, tendency.astype(jnp.bfloat16), 1, 0)
+        modal_ref[:, row, :] = modal * (weight_ref[row] * (1.0 / longitudes))
     table = table_ref[...]
     lane = lax.broadcasted_iota(jnp.int32, table.shape[:1] + (lanes,), 1)
+    spare = jnp.zeros((lanes - used, longitudes), jnp.bfloat16)
     for quarter in range(quarters):
-        block = grid_ref[quarter * used : (quarter + 1) * used, :]
-        block = jnp.concatenate(
-            [block, jnp.zeros((lanes - used, block.shape[1]), block.dtype)], axis=0
-        )
-        sums = contract(table, block, 1, 1)
-        sums = jnp.where(lane < used, sums, count_ref[0])
-        out_ref[:, quarter] = sums.astype(jnp.bfloat16).reshape(wave_count, lat_count, 2, lanes)
+        block = modal_ref[quarter * modes : (quarter + 1) * modes]
+        block = block.reshape(used, longitudes).astype(jnp.bfloat16)
+        sums = contract(table, jnp.concatenate([block, spare], axis=0), 1, 1)
+        sums = jnp.where(lane < used, sums, count_ref[0]).astype(jnp.bfloat16)
+        out_ref[:, quarter] = sums.reshape(wave_count, lat_count, 2, lanes)
 
 
 def selection(count_row, size):
@@ -139,6 +149,30 @@
         out_ref[:, lat] = chosen.reshape(members, 2, lanes)
 
 
+def band_kernel(implicit_ref, legendre_ref, out_ref, band_ref):
+    lat_count, columns, lanes = out_ref.shape
+    _, all_rows, level_count = band_ref.shape
+    rows = all_rows // lat_count
+    waves = legendre_ref.shape[0]
+    for column in range(columns):
+        own = implicit_ref[column // waves, column % waves]
+        band_ref[column] = contract(legendre_ref[column % waves], own, 1, 1)
+    for lat in range(lat_count):
+        for row in range(rows):
+            piece = band_ref[:, lat * rows + row, :].astype(jnp.bfloat16)
+            out_ref[lat, :, row * level_count : (row + 1) * level_count] = piece
+    used = rows * level_count
+    out_ref[:, :, used:] = jnp.zeros((lat_count, columns, lanes - used), jnp.bfloat16)
+
+
+def last_kernel(parts_ref, table_ref, out_ref):
+    level_count, row_count, _ = out_ref.shape
+    parts = parts_ref[...].reshape(table_ref.shape[0], parts_ref.shape[2])
+    sums = contract(parts, table_ref[...], 0, 0)
+    for row in range(row_count):
+        out_ref[:, row, :] = sums[row * level_count : (row + 1) * level_count]
+
+
 def gather_kernel(parts_ref, table_ref, out_ref):
     _, quarters, _, _, lanes = parts_ref.shape
     used = out_ref.shape[0] // quarters
@@ -182,11 +216,6 @@
             "ljpm,mjn->pmln", split_parts, legendre, preferred_element_type=jnp.float32
         )
 
-    def to_grid(received):
-        flat_rows = received.reshape(received.shape[0] * received.shape[1], received.shape[2])
-        result_grid = jnp.dot(flat_rows, backward, preferred_element_type=jnp.float32)
-        return result_grid.reshape(received.shape[0], received.shape[1], longitudes)
-
     def to_implicit(coefficients):
         spectral = to_spectral(
             lax.all_to_all(coefficients, "lat", split_axis=2, concat_axis=1, tiled=True)
@@ -194,12 +223,25 @@
         return implicit_solve(spectral, to_modes, from_modes, divisor)
 
     def to_band_grid(implicit):
-        band_parts = jnp.einsum(
-            "mjn,pmln->ljpm", legendre, implicit, preferred_element_type=jnp.float32
-        )
-        band_parts = band_parts.astype(jnp.bfloat16)
-        band_parts = band_parts.reshape(band_parts.shape[0], band_parts.shape[1], 2 * local_waves)
-        return to_grid(lax.all_to_all(band_parts, "lat", split_axis=1, concat_axis=2, tiled=True))
+        row_lanes = -(-level_count * row_count // 128) * 128
+        blocks = jax.ShapeDtypeStruct((lat_count, 2 * local_waves, row_lanes), jnp.bfloat16)
+        band_blocks = pl.pallas_call(
+            band_kernel,
+            out_shape=blocks,
+            in_specs=[vmem, vmem],
+            out_specs=vmem,
+            scratch_shapes=[
+                pltpu.VMEM((2 * local_waves, lat_count * row_count, level_count), jnp.float32)
+            ],
+            name="band_legendre",
+        )(implicit, legendre)
+        return pl.pallas_call(
+            last_kernel,
+            out_shape=jax.ShapeDtypeStruct((level_count, row_count, longitudes), jnp.float32),
+            in_specs=[vmem, vmem],
+            out_specs=vmem,
+            name="last_fourier",
+        )(lax.all_to_all(band_blocks, "lat", 0, 0, tiled=True), backward)
 
     level_count, row_count = ensemble.shape[1], ensemble.shape[2]
     quarters = traj_count // local_waves
@@ -214,21 +256,22 @@
     own_divisor = lax.dynamic_slice_in_dim(divisor, traj_index % quarters * modes, modes, 0)
     own_inverse = (1.0 / own_divisor).T
 
-    grid_rounded = grid_tendency(ensemble[0], mixing)
-    modal_grid = mix_levels(to_modes, grid_rounded) * lat_scale[None, :, None]
-    modal_grid = modal_grid.astype(jnp.bfloat16)
     outgoing = pl.pallas_call(
-        spread_kernel,
+        first_kernel,
         out_shape=jax.ShapeDtypeStruct(
             (local_waves, quarters, lat_count, 2, lanes), jnp.bfloat16
         ),
-        in_specs=[smem, vmem, vmem],
+        in_specs=[smem, smem, vmem, vmem, vmem, vmem],
         out_specs=vmem,
-        name="spread_fourier",
+        scratch_shapes=[pltpu.VMEM((level_count, row_count, longitudes), jnp.float32)],
+        name="first_fourier",
     )(
         counts.astype(jnp.float32),
+        weights,
         np.ascontiguousarray(pair_forward.T),
-        modal_grid.reshape(level_count * row_count, longitudes),
+        mixing,
+        to_modes.astype(jnp.bfloat16),
+        ensemble[0],
     )
     everyone = ("traj", "lat")
     arrived = lax.all_to_all(

time: 257 us -> 254 us (0.988)
  the two profiles are of different devices: /device:TPU:34 before, /device:TPU:43 now
where the time goes in v3:
time: 254 us; the launch traced here: 253 us
  waiting for transfers between devices  119 us (47%)
  starting transfers between devices  43.5 us (17%)
  blocking collectives  42.2 us (17%)
  Pallas kernels  26.1 us (10%)
  local copies, waits for them, and re-layouts  14.1 us (6%)
  matrix products  4.94 us (2%)
  other arithmetic  2.64 us (1%)
    all_to_all x1, waiting for transfers between devices, local(): lax.all_to_all(band_parts.reshape(traj_count * lat_count, 2, lanes), ever...  42.2 us
    all_to_all x1, blocking collectives, to_band_grid(): lax.all_to_all(band_blocks, 'lat', 0, 0, tiled=True)  42.2 us
    all_to_all x1, waiting for transfers between devices, local(): lax.all_to_all(outgoing.reshape(traj_count * lat_count, 2, lanes), everyo...  40.3 us
    all_to_all x1, waiting for transfers between devices, to_implicit(): lax.all_to_all(coefficients, 'lat', split_axis=2, concat_axis=1, tiled=True)  36.3 us
    all_to_all x1, starting transfers between devices, local(): lax.all_to_all(outgoing.reshape(traj_count * lat_count, 2, lanes), everyo...  23.3 us
    all_to_all x1, starting transfers between devices, local(): lax.all_to_all(band_parts.reshape(traj_count * lat_count, 2, lanes), ever...  13.9 us
    unnamed x22, local copies, waits for them, and re-layouts  9.64 us
    pallas_call x1, Pallas kernels, local(): pl.pallas_call(first_kernel, out_shape=jax.ShapeDtypeStruct((local_waves,...  8.76 us
  transfers between devices with their start and end apart: 3, of which 3 were waited for; matrix products, arithmetic and copies ran while one was open for 1% of the time, Pallas kernels for 0%

profile of v3, /device:TPU:43, one launch (start us, length us, event | category | flops | bytes accessed | tf_op | source)
XLA Modules:
  0.0 253.2 jit_solution(12821805070378345161)
XLA Ops:
  0.7 1.4 convert_element_type.27.to_ref
  2.0 0.0 copy-start
  2.0 0.0 copy-start.6
  2.0 8.8 %first_fourier.1 = bf16[16,4,8,2,384]{4,3,2,1,0:T(2,128)(2,1)} custom-call(f32[1]{0:T(128)S(6)} %convert_element_type.26.count_ref, f32[24]{0:T(128)} %weight_ref.1, bf16[256,384]{1,0:T(8,128)(2,1)} %constant.64.clone.table_ref, bf16[56,56]{1,0:T(8,128)(2,1)} %mixing_ref.1, bf16[56,56]{1,0:T(8,128)(2,1)} %convert_element_type.27.to_ref, f32[56,24,384]{2,1,0:T(8,128)} %bitcast.76), custom_call_target="tpu_custom_call" | custom-call | tf_op jit(solution)/shard_map/first_fourier/pallas_call | solution.py:259
  10.8 23.3 %all-to-all-start = ((bf16[512,2,384]{2,1,0:T(2,128)(2,1)}), bf16[512,2,384]{2,1,0:T(2,128)(2,1)S(1)}, u32[]{:S(2)}, u32[]{:S(2)}) async-start(bf16[512,2,384]{2,1,0:T(2,128)(2,1)} %bitcast.74), calls=%async_computation | async-start | bytes 1572864 | tf_op jit(solution)/shard_map/all_to_all | solution.py:277
  34.0 0.0 copy-start.7
  34.1 0.0 copy-done
  34.1 0.7 copy.37
  34.9 0.6 fusion.30.table_ref
  35.5 0.0 copy-done.6
  35.5 0.1 multiply_add_fusion
  35.6 0.7 divide_bitcast_fusion.inverse_ref
  36.3 40.3 %all-to-all-done = bf16[512,2,384]{2,1,0:T(2,128)(2,1)S(1)} async-done(((bf16[512,2,384]{2,1,0:T(2,128)(2,1)}), bf16[512,2,384]{2,1,0:T(2,128)(2,1)S(1)}, u32[]{:S(2)}, u32[]{:S(2)}) %all-to-all-start) | async-done | bytes 786464 | tf_op jit(solution)/shard_map/all_to_all | solution.py:277
  76.6 0.9 copy-done.1
  77.5 5.5 %wave_solve.1 = bf16[64,8,2,384]{3,2,1,0:T(2,128)(2,1)} custom-call(bf16[64,8,2,384]{3,2,1,0:T(2,128)(2,1)} %bitcast.72, bf16[192,128]{1,0:T(8,128)(2,1)} %fusion.30.table_ref, bf16[128,192]{1,0:T(8,128)(2,1)} %bitcast.77, f32[128,14]{1,0:T(8,128)} %divide_bitcast_fusion.inverse_ref), custom_call_target="tpu_custom_call" | custom-call | tf_op jit(solution)/shard_map/wave_solve/pallas_call | solution.py:280
  83.0 13.9 %all-to-all-start.1 = ((bf16[512,2,384]{2,1,0:T(2,128)(2,1)}), bf16[512,2,384]{2,1,0:T(2,128)(2,1)S(1)}, u32[]{:S(2)}, u32[]{:S(2)}) async-start(bf16[512,2,384]{2,1,0:T(2,128)(2,1)} %bitcast.73), calls=%async_computation.1 | async-start | bytes 1572864 | tf_op jit(solution)/shard_map/all_to_all | solution.py:296
  96.9 0.0 copy-done.7
  96.9 0.0 copy-start.3
  97.0 42.2 %all-to-all-done.1 = bf16[512,2,384]{2,1,0:T(2,128)(2,1)S(1)} async-done(((bf16[512,2,384]{2,1,0:T(2,128)(2,1)}), bf16[512,2,384]{2,1,0:T(2,128)(2,1)S(1)}, u32[]{:S(2)}, u32[]{:S(2)}) %all-to-all-start.1) | async-done | bytes 786464 | tf_op jit(solution)/shard_map/all_to_all | solution.py:296
  139.2 0.9 copy-done.2
  140.1 2.7 %gather_fourier.1 = bf16[1344,384]{1,0:T(8,128)(2,1)} custom-call(bf16[16,4,8,2,384]{4,3,2,1,0:T(2,128)(2,1)} %bitcast.75, bf16[256,384]{1,0:T(8,128)(2,1)} %constant.65.clone.table_ref), custom_call_target="tpu_custom_call" | custom-call | tf_op jit(solution)/shard_map/gather_fourier/pallas_call | solution.py:299
  142.8 1.6 reshape_reshape.3
  144.4 0.0 copy-done.3
  144.4 0.0 copy-start.4
  144.5 0.4 fusion.17
  144.9 0.3 copy-done.4
  145.2 0.4 fusion.21
  145.6 0.4 copy.51
  145.9 0.4 copy.52
  146.3 0.0 copy-start.8
  146.3 0.5 fusion.3
  146.8 0.4 copy-done.8
  147.2 0.5 fusion.6
  147.8 1.1 copy.40
  148.9 3.5 %reshape.75 = bf16[8,2,21504]{2,1,0:T(2,128)(2,1)} reshape(bf16[256,24,56]{2,1,0:T(8,128)(2,1)S(1)} %bitcast.69) | data formatting | bytes 1376256
  152.4 6.3 %all-to-all-start.2 = ((bf16[8,2,21504]{2,1,0:T(2,128)(2,1)}), bf16[8,2,21504]{2,1,0:T(2,128)(2,1)S(1)}, u32[]{:S(2)}, u32[]{:S(2)}) async-start(bf16[8,2,21504]{2,1,0:T(2,128)(2,1)} %reshape.75), calls=%async_computation.2 | async-start | bytes 1376256 | tf_op jit(solution)/shard_map/all_to_all | solution.py:221
  158.8 0.1 copy.45
  158.8 36.3 %all-to-all-done.2 = bf16[8,2,21504]{2,1,0:T(2,128)(2,1)S(1)} async-done(((bf16[8,2,21504]{2,1,0:T(2,128)(2,1)}), bf16[8,2,21504]{2,1,0:T(2,128)(2,1)S(1)}, u32[]{:S(2)}, u32[]{:S(2)}) %all-to-all-start.2) | async-done | bytes 688160 | tf_op jit(solution)/shard_map/all_to_all | solution.py:221
  195.2 2.8 %reshape.76 = bf16[256,24,56]{2,1,0:T(8,128)(2,1)S(1)} reshape(bf16[8,2,21504]{2,1,0:T(2,128)(2,1)S(1)} %all-to-all-done.2) | data formatting | bytes 1376256
  198.0 0.3 copy.42
  198.3 0.0 copy-start.5
  198.3 0.9 fusion.7
  199.2 0.0 copy-done.5
  199.2 1.0 fusion.10
  200.2 1.7 fusion.11.implicit_ref
  201.9 5.7 %band_legendre.1 = bf16[8,32,1408]{2,1,0:T(8,128)(2,1)} custom-call(bf16[2,16,56,128]{3,2,1,0:T(8,128)(2,1)} %fusion.11.implicit_ref, bf16[16,192,128]{2,1,0:T(8,128)(2,1)} %legendre_ref.1), custom_call_target="tpu_custom_call" | custom-call | tf_op jit(solution)/shard_map/band_legendre/pallas_call | solution.py:228
  207.7 42.2 %all_to_all.30.parts_ref = bf16[8,32,1408]{2,1,0:T(8,128)(2,1)} all-to-all(bf16[8,32,1408]{2,1,0:T(8,128)(2,1)} %band_legendre.1), channel_id=1, replica_groups=mesh['traj'=64,'lat'=8] {'lat'}, dimensions={0} | all-to-all | bytes 1441792 | tf_op jit(solution)/shard_map/all_to_all | solution.py:244
  249.9 3.3 %last_fourier.1 = f32[56,24,384]{2,1,0:T(8,128)} custom-call(bf16[8,32,1408]{2,1,0:T(8,128)(2,1)} %all_to_all.30.parts_ref, bf16[256,384]{1,0:T(8,128)(2,1)} %constant.67.clone.table_ref), custom_call_target="tpu_custom_call" | custom-call | tf_op jit(solution)/shard_map/last_fourier/pallas_call | solution.py:238
  (5 shorter events, 0.0 us)
Async XLA Ops:
  2.0 32.1 %copy-start = (bf16[16,192,128]{2,1,0:T(8,128)(2,1)S(1)}, bf16[16,192,128]{2,1,0:T(8,128)(2,1)}, u32[]{:S(2)}) copy-start(bf16[16,192,128]{2,1,0:T(8,128)(2,1)} %legendre_ref.1) | copy-start | bytes 2359300
  2.0 33.5 %copy-start.6 = (f32[56]{0:T(128)S(1)}, f32[56]{0:T(128)}, u32[]{:S(2)}) copy-start(f32[56]{0:T(128)} %param.19) | copy-start | bytes 676
  10.8 65.8 %all-to-all-start = ((bf16[512,2,384]{2,1,0:T(2,128)(2,1)}), bf16[512,2,384]{2,1,0:T(2,128)(2,1)S(1)}, u32[]{:S(2)}, u32[]{:S(2)}) async-start(bf16[512,2,384]{2,1,0:T(2,128)(2,1)} %bitcast.74), calls=%async_computation | async-start | bytes 1572864 | tf_op jit(solution)/shard_map/all_to_all | solution.py:277
  34.0 62.9 %copy-start.7 = (f32[24]{0:T(128)S(1)}, f32[24]{0:T(128)}, u32[]{:S(2)}) copy-start(f32[24]{0:T(128)} %weight_ref.1) | copy-start | bytes 292
  76.6 0.9 copy-start.1
  83.0 56.2 %all-to-all-start.1 = ((bf16[512,2,384]{2,1,0:T(2,128)(2,1)}), bf16[512,2,384]{2,1,0:T(2,128)(2,1)S(1)}, u32[]{:S(2)}, u32[]{:S(2)}) async-start(bf16[512,2,384]{2,1,0:T(2,128)(2,1)} %bitcast.73), calls=%async_computation.1 | async-start | bytes 1572864 | tf_op jit(solution)/shard_map/all_to_all | solution.py:296
  96.9 47.5 %copy-start.3 = (f32[56,56]{1,0:T(8,128)S(1)}, f32[56,56]{1,0:T(8,128)}, u32[]{:S(2)}) copy-start(f32[56,56]{1,0:T(8,128)} %param.18) | copy-start | bytes 37636
  139.2 0.9 copy-start.2
  144.4 0.7 copy-start.4
  146.3 0.9 copy-start.8
  152.4 42.7 %all-to-all-start.2 = ((bf16[8,2,21504]{2,1,0:T(2,128)(2,1)}), bf16[8,2,21504]{2,1,0:T(2,128)(2,1)S(1)}, u32[]{:S(2)}, u32[]{:S(2)}) async-start(bf16[8,2,21504]{2,1,0:T(2,128)(2,1)} %reshape.75), calls=%async_computation.2 | async-start | bytes 1376256 | tf_op jit(solution)/shard_map/all_to_all | solution.py:221
  198.3 0.9 copy-start.5

commit v4 on v3

--- a/solution.py
+++ b/solution.py
@@ -72,17 +72,24 @@
 def first_kernel(
     count_ref, weight_ref, table_ref, mixing_ref, to_ref, grid_ref, out_ref, modal_ref
 ):
-    level_count, row_count, longitudes = grid_ref.shape
+    level_count, groups, _, longitudes = grid_ref.shape
+    row_count = groups * 8
     wave_count, quarters, lat_count, _, lanes = out_ref.shape
     modes = level_count // quarters
     used = modes * row_count
-    mixing, to_modes = mixing_ref[...], to_ref[...]
-    for row in range(row_count):
-        state = grid_ref[:, row, :]
-        mixed = contract(mixing, state.astype(jnp.bfloat16), 1, 0)
-        tendency = state + time_step * (mixed - cubic_rate * state * state * state)
-        modal = contract(to_modes, tendency.astype(jnp.bfloat16), 1, 0)
-        modal_ref[:, row, :] = modal * (weight_ref[row] * (1.0 / longitudes))
+    mixing, to_modes = mixing_ref[...], to_ref[...].astype(jnp.bfloat16)
+
+    def advance(step, carry):
+        for inner in range(8):
+            row = step * 8 + inner
+            state = grid_ref[:, step, inner, :]
+            mixed = contract(mixing, state.astype(jnp.bfloat16), 1, 0)
+            tendency = state + time_step * (mixed - cubic_rate * state * state * state)
+            modal = contract(to_modes, tendency.astype(jnp.bfloat16), 1, 0)
+            modal_ref[:, step, inner, :] = modal * (weight_ref[row] * (1.0 / longitudes))
+        return carry
+
+    lax.fori_loop(0, row_count // 8, advance, 0)
     table = table_ref[...]
     lane = lax.broadcasted_iota(jnp.int32, table.shape[:1] + (lanes,), 1)
     spare = jnp.zeros((lanes - used, longitudes), jnp.bfloat16)
@@ -151,23 +158,31 @@
 
 def band_kernel(implicit_ref, legendre_ref, out_ref, band_ref):
     lat_count, columns, lanes = out_ref.shape
-    _, all_rows, level_count = band_ref.shape
-    rows = all_rows // lat_count
+    _, _, rows, level_count = band_ref.shape
     waves = legendre_ref.shape[0]
     for column in range(columns):
         own = implicit_ref[column // waves, column % waves]
-        band_ref[column] = contract(legendre_ref[column % waves], own, 1, 1)
-    for lat in range(lat_count):
+        band = contract(legendre_ref[column % waves], own, 1, 1)
+        band_ref[column] = band.reshape(lat_count, rows, level_count)
+    used = rows * level_count
+
+    def write(lat, carry):
         for row in range(rows):
-            piece = band_ref[:, lat * rows + row, :].astype(jnp.bfloat16)
+            piece = band_ref[:, lat, row, :].astype(jnp.bfloat16)
             out_ref[lat, :, row * level_count : (row + 1) * level_count] = piece
-    used = rows * level_count
-    out_ref[:, :, used:] = jnp.zeros((lat_count, columns, lanes - used), jnp.bfloat16)
-
-
-def last_kernel(parts_ref, table_ref, out_ref):
+        out_ref[lat, :, used:] = jnp.zeros((columns, lanes - used), jnp.bfloat16)
+        return carry
+
+    lax.fori_loop(0, lat_count, write, 0)
+
+
+def last_kernel(table_ref, *refs):
+    parts_refs, out_ref = refs[:-1], refs[-1]
     level_count, row_count, _ = out_ref.shape
-    parts = parts_ref[...].reshape(table_ref.shape[0], parts_ref.shape[2])
+    size = table_ref.shape[0] // len(parts_refs)
+    parts = jnp.concatenate(
+        [ref[...].reshape(size, ref.shape[2]) for ref in parts_refs], axis=0
+    )
     sums = contract(parts, table_ref[...], 0, 0)
     for row in range(row_count):
         out_ref[:, row, :] = sums[row * level_count : (row + 1) * level_count]
@@ -200,48 +215,40 @@
     degree_count = legendre.shape[2]
     total_waves = local_waves * lat_count
     longitudes = ensemble.shape[3]
+    halves = 2
+    half_waves = local_waves // halves
     columns = np.arange(2 * total_waves)
-    within = columns % (2 * local_waves)
-    wavenumber = columns // (2 * local_waves) * local_waves + within % local_waves
-    component = within // local_waves
-    forward, backward = fourier_tables(wavenumber, component, longitudes)
+    half = columns // (2 * total_waves // halves)
+    within = columns % (2 * half_waves)
+    owner = columns // (2 * half_waves) % lat_count
+    wavenumber = owner * local_waves + half * half_waves + within % half_waves
+    forward, backward = fourier_tables(wavenumber, within // half_waves, longitudes)
     lat_scale = weights / longitudes
     divisor = mode_divisor(mode_rates, degree_count)
     vmem = pl.BlockSpec(memory_space=pltpu.VMEM)
     smem = pl.BlockSpec(memory_space=pltpu.SMEM)
 
-    def to_spectral(received):
-        split_parts = received.reshape(received.shape[0], received.shape[1], 2, local_waves)
-        return jnp.einsum(
-            "ljpm,mjn->pmln", split_parts, legendre, preferred_element_type=jnp.float32
-        )
-
-    def to_implicit(coefficients):
-        spectral = to_spectral(
-            lax.all_to_all(coefficients, "lat", split_axis=2, concat_axis=1, tiled=True)
+    def to_implicit(coefficients, table):
+        received = lax.all_to_all(coefficients, "lat", split_axis=2, concat_axis=1, tiled=True)
+        split_parts = received.reshape(received.shape[0], received.shape[1], 2, half_waves)
+        spectral = jnp.einsum(
+            "ljpm,mjn->pmln", split_parts, table, preferred_element_type=jnp.float32
         )
         return implicit_solve(spectral, to_modes, from_modes, divisor)
 
-    def to_band_grid(implicit):
+    def to_band(implicit, table):
         row_lanes = -(-level_count * row_count // 128) * 128
-        blocks = jax.ShapeDtypeStruct((lat_count, 2 * local_waves, row_lanes), jnp.bfloat16)
         band_blocks = pl.pallas_call(
             band_kernel,
-            out_shape=blocks,
+            out_shape=jax.ShapeDtypeStruct((lat_count, 2 * half_waves, row_lanes), jnp.bfloat16),
             in_specs=[vmem, vmem],
             out_specs=vmem,
             scratch_shapes=[
-                pltpu.VMEM((2 * local_waves, lat_count * row_count, level_count), jnp.float32)
+                pltpu.VMEM((2 * half_waves, lat_count, row_count, level_count), jnp.float32)
             ],
             name="band_legendre",
-        )(implicit, legendre)
-        return pl.pallas_call(
-            last_kernel,
-            out_shape=jax.ShapeDtypeStruct((level_count, row_count, longitudes), jnp.float32),
-            in_specs=[vmem, vmem],
-            out_specs=vmem,
-            name="last_fourier",
-        )(lax.all_to_all(band_blocks, "lat", 0, 0, tiled=True), backward)
+        )(implicit, table)
+        return lax.all_to_all(band_blocks, "lat", 0, 0, tiled=True)
 
     level_count, row_count = ensemble.shape[1], ensemble.shape[2]
     quarters = traj_count // local_waves
@@ -263,15 +270,15 @@
         ),
         in_specs=[smem, smem, vmem, vmem, vmem, vmem],
         out_specs=vmem,
-        scratch_shapes=[pltpu.VMEM((level_count, row_count, longitudes), jnp.float32)],
+        scratch_shapes=[pltpu.VMEM((level_count, row_count // 8, 8, longitudes), jnp.float32)],
         name="first_fourier",
     )(
         counts.astype(jnp.float32),
         weights,
         np.ascontiguousarray(pair_forward.T),
         mixing,
-        to_modes.astype(jnp.bfloat16),
-        ensemble[0],
+        to_modes,
+        ensemble.reshape(level_count, row_count // 8, 8, longitudes),
     )
     everyone = ("traj", "lat")
     arrived = lax.all_to_all(
@@ -304,7 +311,21 @@
         name="gather_fourier",
     )(returned.reshape(local_waves, quarters, lat_count, 2, lanes), pair_backward)
     state_grid = mix_levels(from_modes, modal_grid.reshape(level_count, row_count, longitudes))
-    state_grid = to_band_grid(to_implicit(grid_section(state_grid, mixing, lat_scale, forward)))
+    coefficients = grid_section(state_grid, mixing, lat_scale, forward)
+    share = 2 * total_waves // halves
+    tables = [legendre[at * half_waves : (at + 1) * half_waves] for at in range(halves)]
+    implicit = [
+        to_implicit(coefficients[:, :, at * share : (at + 1) * share], tables[at])
+        for at in range(halves)
+    ]
+    bands = [to_band(implicit[at], tables[at]) for at in range(halves)]
+    state_grid = pl.pallas_call(
+        last_kernel,
+        out_shape=jax.ShapeDtypeStruct((level_count, row_count, longitudes), jnp.float32),
+        in_specs=[vmem] * (halves + 1),
+        out_specs=vmem,
+        name="last_fourier",
+    )(backward, *bands)
     return state_grid[None]
 
 

time: 254 us -> 261 us (1.028)
  the two profiles are of different devices: /device:TPU:43 before, /device:TPU:34 now
where the time goes in v4:
time: 261 us
  waiting for transfers between devices  141 us (54%)
  starting transfers between devices  43.6 us (17%)
  Pallas kernels  29.1 us (11%)
  blocking collectives  23.9 us (9%)
  local copies, waits for them, and re-layouts  15.5 us (6%)
  matrix products  5.68 us (2%)
    all_to_all x1, waiting for transfers between devices, local(): lax.all_to_all(band_parts.reshape(traj_count * lat_count, 2, lanes), ever...  46.2 us
    all_to_all x1, waiting for transfers between devices, local(): lax.all_to_all(outgoing.reshape(traj_count * lat_count, 2, lanes), everyo...  44 us
    all_to_all x2, waiting for transfers between devices, to_implicit(): lax.all_to_all(coefficients, 'lat', split_axis=2, concat_axis=1, tiled=True)  36.1 us
    all_to_all x1, blocking collectives, to_band(): return lax.all_to_all(band_blocks, 'lat', 0, 0, tiled=True)  23.9 us
    all_to_all x1, starting transfers between devices, local(): lax.all_to_all(outgoing.reshape(traj_count * lat_count, 2, lanes), everyo...  23 us
    all_to_all x1, waiting for transfers between devices, to_band(): return lax.all_to_all(band_blocks, 'lat', 0, 0, tiled=True)  14.2 us
    unnamed x26, local copies, waits for them, and re-layouts  10.2 us
    all_to_all x1, starting transfers between devices, local(): lax.all_to_all(band_parts.reshape(traj_count * lat_count, 2, lanes), ever...  10.1 us
  transfers between devices with their start and end apart: 5, of which 5 were waited for; matrix products, arithmetic and copies ran while one was open for 5% of the time, Pallas kernels for 3%

profile of v4, /device:TPU:34, one launch (start us, length us, event | category | flops | bytes accessed | tf_op | source)
XLA Modules:
  0.0 260.6 jit_solution(15455035536171622213)
XLA Ops:
  0.7 9.1 %first_fourier.1 = bf16[16,4,8,2,384]{4,3,2,1,0:T(2,128)(2,1)} custom-call(f32[1]{0:T(128)S(6)} %convert_element_type.28.count_ref, f32[24]{0:T(128)} %weight_ref.1, bf16[256,384]{1,0:T(8,128)(2,1)} %constant.64.clone.table_ref, bf16[56,56]{1,0:T(8,128)(2,1)} %mixing_ref.1, f32[56,56]{1,0:T(8,128)} %to_ref.1, f32[56,3,8,384]{3,2,1,0:T(8,128)} %bitcast.103), custom_call_target="tpu_custom_call" | custom-call | tf_op jit(solution)/shard_map/first_fourier/pallas_call | solution.py:266
  9.8 23.0 %all-to-all-start = ((bf16[512,2,384]{2,1,0:T(2,128)(2,1)}), bf16[512,2,384]{2,1,0:T(2,128)(2,1)S(1)}, u32[]{:S(2)}, u32[]{:S(2)}) async-start(bf16[512,2,384]{2,1,0:T(2,128)(2,1)} %bitcast.101), calls=%async_computation | async-start | bytes 1572864 | tf_op jit(solution)/shard_map/all_to_all | solution.py:284
  32.9 0.7 copy.49
  33.6 0.6 fusion.38.table_ref
  34.2 0.1 multiply_add_fusion
  34.3 0.7 divide_bitcast_fusion.inverse_ref
  35.0 44.0 %all-to-all-done = bf16[512,2,384]{2,1,0:T(2,128)(2,1)S(1)} async-done(((bf16[512,2,384]{2,1,0:T(2,128)(2,1)}), bf16[512,2,384]{2,1,0:T(2,128)(2,1)S(1)}, u32[]{:S(2)}, u32[]{:S(2)}) %all-to-all-start) | async-done | bytes 786464 | tf_op jit(solution)/shard_map/all_to_all | solution.py:284
  79.1 0.9 copy-done.1
  79.9 5.5 %wave_solve.1 = bf16[64,8,2,384]{3,2,1,0:T(2,128)(2,1)} custom-call(bf16[64,8,2,384]{3,2,1,0:T(2,128)(2,1)} %bitcast.93, bf16[192,128]{1,0:T(8,128)(2,1)} %fusion.38.table_ref, bf16[128,192]{1,0:T(8,128)(2,1)} %bitcast.104, f32[128,14]{1,0:T(8,128)} %divide_bitcast_fusion.inverse_ref), custom_call_target="tpu_custom_call" | custom-call | tf_op jit(solution)/shard_map/wave_solve/pallas_call | solution.py:287
  85.4 10.1 %all-to-all-start.1 = ((bf16[512,2,384]{2,1,0:T(2,128)(2,1)}), bf16[512,2,384]{2,1,0:T(2,128)(2,1)S(1)}, u32[]{:S(2)}, u32[]{:S(2)}) async-start(bf16[512,2,384]{2,1,0:T(2,128)(2,1)} %bitcast.94), calls=%async_computation.1 | async-start | bytes 1572864 | tf_op jit(solution)/shard_map/all_to_all | solution.py:303
  95.5 46.2 %all-to-all-done.1 = bf16[512,2,384]{2,1,0:T(2,128)(2,1)S(1)} async-done(((bf16[512,2,384]{2,1,0:T(2,128)(2,1)}), bf16[512,2,384]{2,1,0:T(2,128)(2,1)S(1)}, u32[]{:S(2)}, u32[]{:S(2)}) %all-to-all-start.1) | async-done | bytes 786464 | tf_op jit(solution)/shard_map/all_to_all | solution.py:303
  141.7 0.9 copy-done.2
  142.6 2.7 %gather_fourier.1 = bf16[1344,384]{1,0:T(8,128)(2,1)} custom-call(bf16[16,4,8,2,384]{4,3,2,1,0:T(2,128)(2,1)} %bitcast.102, bf16[256,384]{1,0:T(8,128)(2,1)} %constant.65.clone.table_ref), custom_call_target="tpu_custom_call" | custom-call | tf_op jit(solution)/shard_map/gather_fourier/pallas_call | solution.py:306
  145.4 1.6 reshape_reshape.3
  147.0 0.4 fusion.20
  147.4 0.3 copy-done.5
  147.7 0.4 fusion.28
  148.1 0.4 copy.71
  148.5 0.4 copy.70
  148.8 0.5 fusion.3
  149.3 0.4 copy-done.9
  149.8 0.5 fusion.4
  150.3 0.1 fusion.27
  150.4 0.5 copy.58
  150.9 2.1 reshape.87
  153.0 3.4 %all-to-all-start.4 = ((bf16[8,2,10752]{2,1,0:T(2,128)(2,1)}), bf16[8,2,10752]{2,1,0:T(2,128)(2,1)S(1)}, u32[]{:S(2)}, u32[]{:S(2)}) async-start(bf16[8,2,10752]{2,1,0:T(2,128)(2,1)} %reshape.87), calls=%async_computation.4 | async-start | bytes 688128 | tf_op jit(solution)/shard_map/all_to_all | solution.py:232
  156.4 0.5 copy.52
  156.9 2.1 reshape.85
  159.0 22.4 %all-to-all-done.4 = bf16[8,2,10752]{2,1,0:T(2,128)(2,1)S(1)} async-done(((bf16[8,2,10752]{2,1,0:T(2,128)(2,1)}), bf16[8,2,10752]{2,1,0:T(2,128)(2,1)S(1)}, u32[]{:S(2)}, u32[]{:S(2)}) %all-to-all-start.4) | async-done | bytes 344096 | tf_op jit(solution)/shard_map/all_to_all | solution.py:232
  181.4 3.4 %all-to-all-start.2 = ((bf16[8,2,10752]{2,1,0:T(2,128)(2,1)}), bf16[8,2,10752]{2,1,0:T(2,128)(2,1)S(1)}, u32[]{:S(2)}, u32[]{:S(2)}) async-start(bf16[8,2,10752]{2,1,0:T(2,128)(2,1)} %reshape.85), calls=%async_computation.2 | async-start | bytes 688128 | tf_op jit(solution)/shard_map/all_to_all | solution.py:232
  184.9 1.0 fusion.26
  185.9 1.4 reshape.88
  187.3 0.1 copy.60
  187.4 0.4 convolution_bitcast_fusion.1
  187.8 0.5 fusion.6
  188.3 1.2 fusion.8.implicit_ref
  189.6 4.2 %band_legendre.3 = bf16[8,16,1408]{2,1,0:T(8,128)(2,1)} custom-call(bf16[2,8,56,128]{3,2,1,0:T(8,128)(2,1)} %fusion.8.implicit_ref, bf16[8,192,128]{2,1,0:T(8,128)(2,1)} %get-tuple-element.5.legendre_ref), custom_call_target="tpu_custom_call" | custom-call | tf_op jit(solution)/shard_map/band_legendre/pallas_call | solution.py:241
  193.8 13.7 %all-to-all-done.2 = bf16[8,2,10752]{2,1,0:T(2,128)(2,1)S(1)} async-done(((bf16[8,2,10752]{2,1,0:T(2,128)(2,1)}), bf16[8,2,10752]{2,1,0:T(2,128)(2,1)S(1)}, u32[]{:S(2)}, u32[]{:S(2)}) %all-to-all-start.2) | async-done | bytes 344096 | tf_op jit(solution)/shard_map/all_to_all | solution.py:232
  207.5 3.7 %all-to-all-start.5 = ((bf16[8,16,1408]{2,1,0:T(8,128)(2,1)}), bf16[8,16,1408]{2,1,0:T(8,128)(2,1)S(1)}, u32[]{:S(2)}, u32[]{:S(2)}) async-start(bf16[8,16,1408]{2,1,0:T(8,128)(2,1)} %band_legendre.3), calls=%async_computation.5 | async-start | bytes 720896 | tf_op jit(solution)/shard_map/all_to_all | solution.py:251
  211.2 1.4 reshape.86
  212.6 0.1 copy.54
  212.7 0.4 convolution_bitcast_fusion.3
  213.1 0.6 fusion.5
  213.7 1.3 fusion.7.implicit_ref
  214.9 4.2 %band_legendre.2 = bf16[8,16,1408]{2,1,0:T(8,128)(2,1)} custom-call(bf16[2,8,56,128]{3,2,1,0:T(8,128)(2,1)} %fusion.7.implicit_ref, bf16[8,192,128]{2,1,0:T(8,128)(2,1)} %get-tuple-element.6.legendre_ref), custom_call_target="tpu_custom_call" | custom-call | tf_op jit(solution)/shard_map/band_legendre/pallas_call | solution.py:241
  219.1 14.2 %all-to-all-done.5.refs_1_ = bf16[8,16,1408]{2,1,0:T(8,128)(2,1)S(1)} async-done(((bf16[8,16,1408]{2,1,0:T(8,128)(2,1)}), bf16[8,16,1408]{2,1,0:T(8,128)(2,1)S(1)}, u32[]{:S(2)}, u32[]{:S(2)}) %all-to-all-start.5) | async-done | bytes 360480 | tf_op jit(solution)/shard_map/all_to_all | solution.py:251
  233.3 23.9 %all_to_all.50.refs_0_ = bf16[8,16,1408]{2,1,0:T(8,128)(2,1)} all-to-all(bf16[8,16,1408]{2,1,0:T(8,128)(2,1)} %band_legendre.2), channel_id=1, replica_groups=mesh['traj'=64,'lat'=8] {'lat'}, dimensions={0} | all-to-all | bytes 720896 | tf_op jit(solution)/shard_map/all_to_all | solution.py:251
  257.2 3.4 %last_fourier.1 = f32[56,24,384]{2,1,0:T(8,128)} custom-call(bf16[256,384]{1,0:T(8,128)(2,1)} %constant.67.clone.table_ref, bf16[8,16,1408]{2,1,0:T(8,128)(2,1)} %all_to_all.50.refs_0_, bf16[8,16,1408]{2,1,0:T(8,128)(2,1)} %copy-done.3), custom_call_target="tpu_custom_call" | custom-call | tf_op jit(solution)/shard_map/last_fourier/pallas_call | solution.py:322
  (20 shorter events, 0.1 us)
Async XLA Ops:
  0.7 32.2 %copy-start = (bf16[16,192,128]{2,1,0:T(8,128)(2,1)S(1)}, bf16[16,192,128]{2,1,0:T(8,128)(2,1)}, u32[]{:S(2)}) copy-start(bf16[16,192,128]{2,1,0:T(8,128)(2,1)} %param.16) | copy-start | bytes 2359300
  0.7 33.6 %copy-start.7 = (f32[56]{0:T(128)S(1)}, f32[56]{0:T(128)}, u32[]{:S(2)}) copy-start(f32[56]{0:T(128)} %param.19) | copy-start | bytes 676
  9.8 69.3 %all-to-all-start = ((bf16[512,2,384]{2,1,0:T(2,128)(2,1)}), bf16[512,2,384]{2,1,0:T(2,128)(2,1)S(1)}, u32[]{:S(2)}, u32[]{:S(2)}) async-start(bf16[512,2,384]{2,1,0:T(2,128)(2,1)} %bitcast.101), calls=%async_computation | async-start | bytes 1572864 | tf_op jit(solution)/shard_map/all_to_all | solution.py:284
  32.8 62.7 %copy-start.8 = (f32[24]{0:T(128)S(1)}, f32[24]{0:T(128)}, u32[]{:S(2)}) copy-start(f32[24]{0:T(128)} %weight_ref.1) | copy-start | bytes 292
  79.1 0.9 copy-start.1
  85.4 56.3 %all-to-all-start.1 = ((bf16[512,2,384]{2,1,0:T(2,128)(2,1)}), bf16[512,2,384]{2,1,0:T(2,128)(2,1)S(1)}, u32[]{:S(2)}, u32[]{:S(2)}) async-start(bf16[512,2,384]{2,1,0:T(2,128)(2,1)} %bitcast.94), calls=%async_computation.1 | async-start | bytes 1572864 | tf_op jit(solution)/shard_map/all_to_all | solution.py:303
  95.5 51.5 %copy-start.4 = (f32[56,56]{1,0:T(8,128)S(1)}, f32[56,56]{1,0:T(8,128)}, u32[]{:S(2)}) copy-start(f32[56,56]{1,0:T(8,128)} %param.18) | copy-start | bytes 37636
  141.7 0.9 copy-start.2
  147.0 0.7 copy-start.5
  148.8 0.9 copy-start.9
  153.0 28.4 %all-to-all-start.4 = ((bf16[8,2,10752]{2,1,0:T(2,128)(2,1)}), bf16[8,2,10752]{2,1,0:T(2,128)(2,1)S(1)}, u32[]{:S(2)}, u32[]{:S(2)}) async-start(bf16[8,2,10752]{2,1,0:T(2,128)(2,1)} %reshape.87), calls=%async_computation.4 | async-start | bytes 688128 | tf_op jit(solution)/shard_map/all_to_all | solution.py:232
  181.4 26.1 %all-to-all-start.2 = ((bf16[8,2,10752]{2,1,0:T(2,128)(2,1)}), bf16[8,2,10752]{2,1,0:T(2,128)(2,1)S(1)}, u32[]{:S(2)}, u32[]{:S(2)}) async-start(bf16[8,2,10752]{2,1,0:T(2,128)(2,1)} %reshape.85), calls=%async_computation.2 | async-start | bytes 688128 | tf_op jit(solution)/shard_map/all_to_all | solution.py:232
  185.9 1.9 copy-start.6
  207.5 25.8 %all-to-all-start.5 = ((bf16[8,16,1408]{2,1,0:T(8,128)(2,1)}), bf16[8,16,1408]{2,1,0:T(8,128)(2,1)S(1)}, u32[]{:S(2)}, u32[]{:S(2)}) async-start(bf16[8,16,1408]{2,1,0:T(8,128)(2,1)} %band_legendre.3), calls=%async_computation.5 | async-start | bytes 720896 | tf_op jit(solution)/shard_map/all_to_all | solution.py:251
  233.3 23.9 %copy-start.3 = (bf16[8,16,1408]{2,1,0:T(8,128)(2,1)}, bf16[8,16,1408]{2,1,0:T(8,128)(2,1)S(1)}, u32[]{:S(2)}) copy-start(bf16[8,16,1408]{2,1,0:T(8,128)(2,1)S(1)} %all-to-all-done.5.refs_1_) | copy-start | bytes 1081348

commit v5 on v3

--- a/solution.py
+++ b/solution.py
@@ -72,17 +72,24 @@
 def first_kernel(
     count_ref, weight_ref, table_ref, mixing_ref, to_ref, grid_ref, out_ref, modal_ref
 ):
-    level_count, row_count, longitudes = grid_ref.shape
+    level_count, groups, _, longitudes = grid_ref.shape
+    row_count = groups * 8
     wave_count, quarters, lat_count, _, lanes = out_ref.shape
     modes = level_count // quarters
     used = modes * row_count
-    mixing, to_modes = mixing_ref[...], to_ref[...]
-    for row in range(row_count):
-        state = grid_ref[:, row, :]
-        mixed = contract(mixing, state.astype(jnp.bfloat16), 1, 0)
-        tendency = state + time_step * (mixed - cubic_rate * state * state * state)
-        modal = contract(to_modes, tendency.astype(jnp.bfloat16), 1, 0)
-        modal_ref[:, row, :] = modal * (weight_ref[row] * (1.0 / longitudes))
+    mixing, to_modes = mixing_ref[...], to_ref[...].astype(jnp.bfloat16)
+
+    def advance(step, carry):
+        for inner in range(8):
+            row = step * 8 + inner
+            state = grid_ref[:, step, inner, :]
+            mixed = contract(mixing, state.astype(jnp.bfloat16), 1, 0)
+            tendency = state + time_step * (mixed - cubic_rate * state * state * state)
+            modal = contract(to_modes, tendency.astype(jnp.bfloat16), 1, 0)
+            modal_ref[:, step, inner, :] = modal * (weight_ref[row] * (1.0 / longitudes))
+        return carry
+
+    lax.fori_loop(0, row_count // 8, advance, 0)
     table = table_ref[...]
     lane = lax.broadcasted_iota(jnp.int32, table.shape[:1] + (lanes,), 1)
     spare = jnp.zeros((lanes - used, longitudes), jnp.bfloat16)
@@ -185,10 +192,10 @@
 
 def implicit_solve(spectral, to_modes, from_modes, divisor):
     modal = (
-        jnp.einsum("kl,pmln->pmkn", to_modes, spectral, precision=lax.Precision.HIGHEST)
+        jnp.einsum("kl,pmln->pmkn", to_modes, spectral, precision=lax.Precision.HIGH)
         / divisor[None, None]
     )
-    return jnp.einsum("lk,pmkn->pmln", from_modes, modal, precision=lax.Precision.HIGHEST).astype(
+    return jnp.einsum("lk,pmkn->pmln", from_modes, modal, precision=lax.Precision.HIGH).astype(
         jnp.bfloat16
     )
 
@@ -263,15 +270,15 @@
         ),
         in_specs=[smem, smem, vmem, vmem, vmem, vmem],
         out_specs=vmem,
-        scratch_shapes=[pltpu.VMEM((level_count, row_count, longitudes), jnp.float32)],
+        scratch_shapes=[pltpu.VMEM((level_count, row_count // 8, 8, longitudes), jnp.float32)],
         name="first_fourier",
     )(
         counts.astype(jnp.float32),
         weights,
         np.ascontiguousarray(pair_forward.T),
         mixing,
-        to_modes.astype(jnp.bfloat16),
-        ensemble[0],
+        to_modes,
+        ensemble.reshape(level_count, row_count // 8, 8, longitudes),
     )
     everyone = ("traj", "lat")
     arrived = lax.all_to_all(

time: 254 us -> 251 us (0.988)
  the two profiles are of different devices: /device:TPU:43 before, /device:TPU:34 now
where the time goes in v5:
time: 251 us; the launch traced here: 250 us
  waiting for transfers between devices  130 us (52%)
  blocking collectives  36.9 us (15%)
  starting transfers between devices  36.8 us (15%)
  Pallas kernels  26.4 us (11%)
  local copies, waits for them, and re-layouts  14.1 us (6%)
  matrix products  4.06 us (2%)
    all_to_all x1, waiting for transfers between devices, local(): lax.all_to_all(band_parts.reshape(traj_count * lat_count, 2, lanes), ever...  46.2 us
    all_to_all x1, waiting for transfers between devices, local(): lax.all_to_all(outgoing.reshape(traj_count * lat_count, 2, lanes), everyo...  44 us
    all_to_all x1, waiting for transfers between devices, to_implicit(): lax.all_to_all(coefficients, 'lat', split_axis=2, concat_axis=1, tiled=True)  39.4 us
    all_to_all x1, blocking collectives, to_band_grid(): lax.all_to_all(band_blocks, 'lat', 0, 0, tiled=True)  36.9 us
    all_to_all x1, starting transfers between devices, local(): lax.all_to_all(outgoing.reshape(traj_count * lat_count, 2, lanes), everyo...  23 us
    all_to_all x1, starting transfers between devices, local(): lax.all_to_all(band_parts.reshape(traj_count * lat_count, 2, lanes), ever...  10 us
    unnamed x22, local copies, waits for them, and re-layouts  9.65 us
    pallas_call x1, Pallas kernels, local(): pl.pallas_call(first_kernel, out_shape=jax.ShapeDtypeStruct((local_waves,...  9.09 us
  transfers between devices with their start and end apart: 3, of which 3 were waited for; matrix products, arithmetic and copies ran while one was open for 1% of the time, Pallas kernels for 0%

profile of v5, /device:TPU:34, one launch (start us, length us, event | category | flops | bytes accessed | tf_op | source)
XLA Modules:
  0.0 250.1 jit_solution(16525562377367558735)
XLA Ops:
  0.7 0.0 copy-start
  0.7 0.0 copy-start.6
  0.7 9.1 %first_fourier.1 = bf16[16,4,8,2,384]{4,3,2,1,0:T(2,128)(2,1)} custom-call(f32[1]{0:T(128)S(6)} %convert_element_type.23.count_ref, f32[24]{0:T(128)} %weight_ref.1, bf16[256,384]{1,0:T(8,128)(2,1)} %constant.64.clone.table_ref, bf16[56,56]{1,0:T(8,128)(2,1)} %mixing_ref.1, f32[56,56]{1,0:T(8,128)} %to_ref.1, f32[56,3,8,384]{3,2,1,0:T(8,128)} %bitcast.76), custom_call_target="tpu_custom_call" | custom-call | tf_op jit(solution)/shard_map/first_fourier/pallas_call | solution.py:266
  9.8 23.0 %all-to-all-start = ((bf16[512,2,384]{2,1,0:T(2,128)(2,1)}), bf16[512,2,384]{2,1,0:T(2,128)(2,1)S(1)}, u32[]{:S(2)}, u32[]{:S(2)}) async-start(bf16[512,2,384]{2,1,0:T(2,128)(2,1)} %bitcast.74), calls=%async_computation | async-start | bytes 1572864 | tf_op jit(solution)/shard_map/all_to_all | solution.py:284
  32.8 0.0 copy-start.7
  32.8 0.0 copy-done
  32.9 0.7 copy.37
  33.6 0.6 fusion.30.table_ref
  34.2 0.0 copy-done.6
  34.2 0.1 multiply_add_fusion
  34.3 0.7 divide_bitcast_fusion.inverse_ref
  35.0 44.0 %all-to-all-done = bf16[512,2,384]{2,1,0:T(2,128)(2,1)S(1)} async-done(((bf16[512,2,384]{2,1,0:T(2,128)(2,1)}), bf16[512,2,384]{2,1,0:T(2,128)(2,1)S(1)}, u32[]{:S(2)}, u32[]{:S(2)}) %all-to-all-start) | async-done | bytes 786464 | tf_op jit(solution)/shard_map/all_to_all | solution.py:284
  79.1 0.0 copy-start.1
  79.1 0.9 copy-done.1
  79.9 5.5 %wave_solve.1 = bf16[64,8,2,384]{3,2,1,0:T(2,128)(2,1)} custom-call(bf16[64,8,2,384]{3,2,1,0:T(2,128)(2,1)} %bitcast.72, bf16[192,128]{1,0:T(8,128)(2,1)} %fusion.30.table_ref, bf16[128,192]{1,0:T(8,128)(2,1)} %bitcast.77, f32[128,14]{1,0:T(8,128)} %divide_bitcast_fusion.inverse_ref), custom_call_target="tpu_custom_call" | custom-call | tf_op jit(solution)/shard_map/wave_solve/pallas_call | solution.py:287
  85.5 10.0 %all-to-all-start.1 = ((bf16[512,2,384]{2,1,0:T(2,128)(2,1)}), bf16[512,2,384]{2,1,0:T(2,128)(2,1)S(1)}, u32[]{:S(2)}, u32[]{:S(2)}) async-start(bf16[512,2,384]{2,1,0:T(2,128)(2,1)} %bitcast.73), calls=%async_computation.1 | async-start | bytes 1572864 | tf_op jit(solution)/shard_map/all_to_all | solution.py:303
  95.5 0.0 copy-done.7
  95.5 0.0 copy-start.3
  95.5 46.2 %all-to-all-done.1 = bf16[512,2,384]{2,1,0:T(2,128)(2,1)S(1)} async-done(((bf16[512,2,384]{2,1,0:T(2,128)(2,1)}), bf16[512,2,384]{2,1,0:T(2,128)(2,1)S(1)}, u32[]{:S(2)}, u32[]{:S(2)}) %all-to-all-start.1) | async-done | bytes 786464 | tf_op jit(solution)/shard_map/all_to_all | solution.py:303
  141.8 0.9 copy-done.2
  142.7 2.7 %gather_fourier.1 = bf16[1344,384]{1,0:T(8,128)(2,1)} custom-call(bf16[16,4,8,2,384]{4,3,2,1,0:T(2,128)(2,1)} %bitcast.75, bf16[256,384]{1,0:T(8,128)(2,1)} %constant.65.clone.table_ref), custom_call_target="tpu_custom_call" | custom-call | tf_op jit(solution)/shard_map/gather_fourier/pallas_call | solution.py:306
  145.4 1.6 reshape_reshape.3
  147.0 0.0 copy-done.3
  147.0 0.0 copy-start.4
  147.0 0.4 fusion.17
  147.4 0.3 copy-done.4
  147.7 0.4 fusion.21
  148.2 0.4 copy.51
  148.5 0.4 copy.52
  148.9 0.0 copy-start.8
  148.9 0.5 fusion.3
  149.4 0.4 copy-done.8
  149.8 0.5 fusion.6
  150.3 1.1 copy.40
  151.5 3.5 %reshape.79 = bf16[8,2,21504]{2,1,0:T(2,128)(2,1)} reshape(bf16[256,24,56]{2,1,0:T(8,128)(2,1)S(1)} %bitcast.69) | data formatting | bytes 1376256
  155.0 3.8 %all-to-all-start.2 = ((bf16[8,2,21504]{2,1,0:T(2,128)(2,1)}), bf16[8,2,21504]{2,1,0:T(2,128)(2,1)S(1)}, u32[]{:S(2)}, u32[]{:S(2)}) async-start(bf16[8,2,21504]{2,1,0:T(2,128)(2,1)} %reshape.79), calls=%async_computation.2 | async-start | bytes 1376256 | tf_op jit(solution)/shard_map/all_to_all | solution.py:228
  158.8 0.1 copy.45
  158.9 39.4 %all-to-all-done.2 = bf16[8,2,21504]{2,1,0:T(2,128)(2,1)S(1)} async-done(((bf16[8,2,21504]{2,1,0:T(2,128)(2,1)}), bf16[8,2,21504]{2,1,0:T(2,128)(2,1)S(1)}, u32[]{:S(2)}, u32[]{:S(2)}) %all-to-all-start.2) | async-done | bytes 688160 | tf_op jit(solution)/shard_map/all_to_all | solution.py:228
  198.2 2.8 %reshape.80 = bf16[256,24,56]{2,1,0:T(8,128)(2,1)S(1)} reshape(bf16[8,2,21504]{2,1,0:T(2,128)(2,1)S(1)} %all-to-all-done.2) | data formatting | bytes 1376256
  201.1 0.3 copy.42
  201.4 0.0 copy-start.5
  201.4 0.9 fusion.7
  202.3 0.0 copy-done.5
  202.3 0.5 fusion.10
  202.8 1.3 fusion.11.implicit_ref
  204.1 5.7 %band_legendre.1 = bf16[8,32,1408]{2,1,0:T(8,128)(2,1)} custom-call(bf16[2,16,56,128]{3,2,1,0:T(8,128)(2,1)} %fusion.11.implicit_ref, bf16[16,192,128]{2,1,0:T(8,128)(2,1)} %legendre_ref.1), custom_call_target="tpu_custom_call" | custom-call | tf_op jit(solution)/shard_map/band_legendre/pallas_call | solution.py:235
  209.9 36.9 %all_to_all.30.parts_ref = bf16[8,32,1408]{2,1,0:T(8,128)(2,1)} all-to-all(bf16[8,32,1408]{2,1,0:T(8,128)(2,1)} %band_legendre.1), channel_id=1, replica_groups=mesh['traj'=64,'lat'=8] {'lat'}, dimensions={0} | all-to-all | bytes 1441792 | tf_op jit(solution)/shard_map/all_to_all | solution.py:251
  246.8 3.3 %last_fourier.1 = f32[56,24,384]{2,1,0:T(8,128)} custom-call(bf16[8,32,1408]{2,1,0:T(8,128)(2,1)} %all_to_all.30.parts_ref, bf16[256,384]{1,0:T(8,128)(2,1)} %constant.67.clone.table_ref), custom_call_target="tpu_custom_call" | custom-call | tf_op jit(solution)/shard_map/last_fourier/pallas_call | solution.py:245
  (4 shorter events, 0.0 us)
Async XLA Ops:
  0.7 32.2 %copy-start = (bf16[16,192,128]{2,1,0:T(8,128)(2,1)S(1)}, bf16[16,192,128]{2,1,0:T(8,128)(2,1)}, u32[]{:S(2)}) copy-start(bf16[16,192,128]{2,1,0:T(8,128)(2,1)} %legendre_ref.1) | copy-start | bytes 2359300
  0.7 33.6 %copy-start.6 = (f32[56]{0:T(128)S(1)}, f32[56]{0:T(128)}, u32[]{:S(2)}) copy-start(f32[56]{0:T(128)} %param.19) | copy-start | bytes 676
  9.8 69.3 %all-to-all-start = ((bf16[512,2,384]{2,1,0:T(2,128)(2,1)}), bf16[512,2,384]{2,1,0:T(2,128)(2,1)S(1)}, u32[]{:S(2)}, u32[]{:S(2)}) async-start(bf16[512,2,384]{2,1,0:T(2,128)(2,1)} %bitcast.74), calls=%async_computation | async-start | bytes 1572864 | tf_op jit(solution)/shard_map/all_to_all | solution.py:284
  32.8 62.7 %copy-start.7 = (f32[24]{0:T(128)S(1)}, f32[24]{0:T(128)}, u32[]{:S(2)}) copy-start(f32[24]{0:T(128)} %weight_ref.1) | copy-start | bytes 292
  79.1 0.9 copy-start.1
  85.5 56.3 %all-to-all-start.1 = ((bf16[512,2,384]{2,1,0:T(2,128)(2,1)}), bf16[512,2,384]{2,1,0:T(2,128)(2,1)S(1)}, u32[]{:S(2)}, u32[]{:S(2)}) async-start(bf16[512,2,384]{2,1,0:T(2,128)(2,1)} %bitcast.73), calls=%async_computation.1 | async-start | bytes 1572864 | tf_op jit(solution)/shard_map/all_to_all | solution.py:303
  95.5 51.5 %copy-start.3 = (f32[56,56]{1,0:T(8,128)S(1)}, f32[56,56]{1,0:T(8,128)}, u32[]{:S(2)}) copy-start(f32[56,56]{1,0:T(8,128)} %param.18) | copy-start | bytes 37636
  141.8 0.9 copy-start.2
  147.0 0.7 copy-start.4
  148.9 0.9 copy-start.8
  155.0 43.2 %all-to-all-start.2 = ((bf16[8,2,21504]{2,1,0:T(2,128)(2,1)}), bf16[8,2,21504]{2,1,0:T(2,128)(2,1)S(1)}, u32[]{:S(2)}, u32[]{:S(2)}) async-start(bf16[8,2,21504]{2,1,0:T(2,128)(2,1)} %reshape.79), calls=%async_computation.2 | async-start | bytes 1376256 | tf_op jit(solution)/shard_map/all_to_all | solution.py:228
  201.4 0.9 copy-start.5
